TPU v7x, 512 devices: a whole 4x4x16 slice. The times are simulated.
512 devices in a mesh: row: 4 (over y), col: 16 (over z), dep: 8 (over x, core).
Axes of the slice: x: 4, y: 4, z: 16, core: 2. Of those that a mesh axis runs over, the one named last changes fastest.
Arguments:
- matrix: float32 [16384, 16384], P('row', ('col', 'dep')), may hold values from -6 to 6
- vectors: float32 [64, 16384], P(None, ('row', 'col')), may hold values from -0.09375 to 0.09375
Outputs:
- reduced: float32 [16384, 16384], P('row', ('col', 'dep'))
All inputs are finite; a program needn't handle non-finite values.
Results may differ from a plain program's by a relative error of at most 0.0001.
Values sent between devices are 32-bit elements; how exact they have to be, the bound alone decides.
No kernel may reach another device: no remote copies, remote signals or barrier semaphores. Data moves between devices by JAX's collectives and lax.ppermute only.
A program may use at most 64 MiB of HBM per device.

v0:
```python
import jax
import jax.numpy as jnp
from jax import lax
from jax.sharding import Mesh
from jax.sharding import PartitionSpec as P

DEP = ("dep_0", "dep_1")
COL_DEP = ("col", "dep_0", "dep_1")


highest = lax.Precision.HIGHEST


def sent_to_all(array, axis):
    copies = jnp.broadcast_to(array, (lax.axis_size(axis), *array.shape))
    return lax.all_to_all(copies, axis, split_axis=0, concat_axis=0, tiled=True)


def joined_along(pieces, dim):
    pieces = jnp.moveaxis(pieces, 0, dim)
    lengths = pieces.shape
    return pieces.reshape(*lengths[:dim], lengths[dim] * lengths[dim + 1], *lengths[dim + 2 :])


def gather_directly(array, axis, dim):
    pieces = sent_to_all(array, axis)
    return joined_along(pieces, dim)


def from_root(array, axis, root):
    return lax.dynamic_index_in_dim(lax.all_gather(array, axis), root, 0, keepdims=False)


def taken_together(array, axis):
    return sent_to_all(array, axis).sum(axis=0)


def padded_to(lines, devices):
    spare = -len(lines) % devices
    return jnp.pad(lines, [(0, spare)] + [(0, 0)] * (lines.ndim - 1))


def whole_of(array, axes, dim):
    far, near = axes
    pieces = sent_to_all(sent_to_all(array, far), near)
    return joined_along(pieces.swapaxes(0, 1).reshape(-1, *array.shape), dim)


def cut_along(array, dim, devices):
    lengths = array.shape
    pieces = array.reshape(*lengths[:dim], devices, lengths[dim] // devices, *lengths[dim + 1 :])
    return jnp.moveaxis(pieces, dim, 0)


def sent_and_summed(array, axis, dim):
    devices = lax.axis_size(axis)
    pieces = lax.all_to_all(cut_along(array, dim, devices), axis, 0, 0, tiled=True)
    return jnp.sum(pieces, axis=0)


def sum_in_two_steps(array, axes, dim):
    far, near = axes
    own = sent_and_summed(cut_along(array, dim, lax.axis_size(far)), near, dim + 1)
    return jnp.sum(lax.all_to_all(own, far, 0, 0, tiled=True), axis=0)


def sum_by_parts(array, axes):
    lines = array.reshape(-1)
    padded = padded_to(lines, lax.axis_size(axes[0]) * lax.axis_size(axes[1]))
    whole = whole_of(sum_in_two_steps(padded, axes, 0), axes, 0)
    return lax.slice_in_dim(whole, 0, len(lines)).reshape(array.shape)


def contract(left, right, dims):
    return lax.dot_general(left, right, (dims, ((), ())), precision=highest)


def mask_vectors(values, first_row):
    panel_width, row_count = values.shape
    positions = first_row + lax.iota(jnp.int32, row_count)[None, :]
    reflector = lax.iota(jnp.int32, panel_width)[:, None]
    filler = jnp.where(positions == reflector + 1, 1.0, 0.0).astype(values.dtype)
    return jnp.where(positions > reflector + 1, values, filler)


def make_factor(gram):
    size_b = gram.shape[0]
    half_diag = 0.5 * jnp.diagonal(gram)
    scaled = jnp.triu(gram, 1) / half_diag[:, None]
    identity = jnp.eye(size_b, dtype=gram.dtype)
    inverse = identity - scaled
    powered = scaled
    for level in range((size_b - 1).bit_length() - 1):
        powered = jnp.dot(powered, powered, precision=highest)
        inverse = jnp.dot(inverse, identity + powered, precision=highest)
    return inverse / half_diag[None, :]


def on_device(matrix, vectors):
    rows_dev, cols_dev = matrix.shape
    row_index = lax.axis_index("row")
    gathered = gather_directly(vectors, "col", 1)
    row_vectors = mask_vectors(gathered, row_index * rows_dev)
    col_block = lax.axis_index("col") * lax.axis_size(DEP) + lax.axis_index(DEP)
    offset = col_block * cols_dev - row_index * rows_dev
    local_piece = lax.dynamic_slice_in_dim(row_vectors, offset, cols_dev, 1)
    owner_row = col_block * cols_dev // rows_dev
    col_vectors = from_root(local_piece, "row", owner_row)
    gram_part = contract(row_vectors, row_vectors, ((1,), (1,)))
    gram_total = taken_together(gram_part, "row")
    factor = make_factor(gram_total)
    partial_value = contract(col_vectors, matrix, ((1,), (1,)))
    summed = sum_by_parts(partial_value, (("col", "dep_0"), "dep_1"))
    update = contract(factor, summed, ((0,), (0,)))
    right_done = matrix - contract(update, col_vectors, ((0,), (0,)))
    left_terms = taken_together(contract(row_vectors, right_done, ((1,), (0,))), "row")
    scaled_terms = contract(factor, left_terms, ((0,), (0,)))
    return right_done - contract(row_vectors, scaled_terms, ((0,), (0,)))


def solution(mesh):
    torus = Mesh(
        mesh.devices.reshape(mesh.shape["row"], mesh.shape["col"], 4, 2),
        ("row", "col", "dep_0", "dep_1"),
    )
    placed = (P("row", COL_DEP), P(None, ("row", "col")))
    return jax.shard_map(
        on_device, mesh=torus, in_specs=placed, out_specs=P("row", COL_DEP), check_vma=False
    )
```

profile of v0, /device:TPU:1, one launch (start us, length us, event | category | flops | bytes accessed | tf_op | source)
XLA Modules:
  0.0 205.7 jit_solution(6435030391687152232)
XLA Ops:
  0.0 1.9 broadcast_in_dim.40
  1.9 15.7 %all-to-all-start = ((f32[16,64,256]{2,1,0:T(8,128)}), f32[16,64,256]{2,1,0:T(8,128)S(1)}, u32[]{:S(2)}, u32[]{:S(2)}) async-start(f32[16,64,256]{2,1,0:T(8,128)} %broadcast_in_dim.40), calls=%async_computation | async-start | bytes 2097152 | tf_op jit(solution)/shard_map/all_to_all | solution.py:16
  17.7 44.8 %all-to-all-done = f32[16,64,256]{2,1,0:T(8,128)S(1)} async-done(((f32[16,64,256]{2,1,0:T(8,128)}), f32[16,64,256]{2,1,0:T(8,128)S(1)}, u32[]{:S(2)}, u32[]{:S(2)}) %all-to-all-start) | async-done | bytes 1048608 | tf_op jit(solution)/shard_map/all_to_all | solution.py:16
  62.5 1.3 convolution_bitcast_fusion.1
  63.8 0.7 reshape.81
  64.7 0.2 select_select_fusion
  64.9 9.8 %all-gather = f32[256,128]{1,0:T(8,128)S(1)} all-gather(f32[64,128]{1,0:T(8,128)S(1)} %constant_dynamic-slice_fusion), channel_id=2, replica_groups=mesh['row'=4,'col'=16,'dep_0'=4,'dep_1'=2] {'row'}, dimensions={0}, use_global_device_ids=true | all-gather | bytes 163840 | tf_op jit(solution)/shard_map/all_gather | solution.py:31
  74.7 2.4 %convolution_bitcast_fusion = f32[2,64,2048]{2,1,0:T(8,128)S(1)} fusion(f32[2,2048,128]{2,1,0:T(8,128)S(1)} %bitcast.48, f32[4,64,128]{2,1,0:T(8,128)S(1)} %bitcast.54, s32[]{:T(128)S(6)} %select_n.43), kind=kOutput, calls=%fused_computation.3 | convolution fusion | flops 402653184 | bytes 3178500 | tf_op jit(solution)/shard_map/dot_general | solution.py:75
  77.1 13.2 %all_to_all.43 = f32[2,64,2048]{2,1,0:T(8,128)S(1)} all-to-all(f32[2,64,2048]{2,1,0:T(8,128)S(1)} %convolution_bitcast_fusion), channel_id=1, replica_groups=mesh['row'=4,'col'=16,'dep_0'=4,'dep_1'=2] {'dep_1'}, dimensions={0} | all-to-all | bytes 2097152 | tf_op jit(solution)/shard_map/all_to_all | solution.py:57
  90.2 3.5 %all-to-all-start.1 = ((f32[4,1,4096]{2,1,0:T(1,128)}), f32[4,1,4096]{2,1,0:T(1,128)S(1)}, u32[]{:S(2)}, u32[]{:S(2)}) async-start(f32[4,1,4096]{2,1,0:T(1,128)} %reshape.81), calls=%async_computation.1 | async-start | bytes 131072 | tf_op jit(solution)/shard_map/all_to_all | solution.py:16
  93.8 1.2 all_to_all.30
  95.0 3.2 %all-to-all-done.1 = f32[4,1,4096]{2,1,0:T(1,128)S(1)} async-done(((f32[4,1,4096]{2,1,0:T(1,128)}), f32[4,1,4096]{2,1,0:T(1,128)S(1)}, u32[]{:S(2)}, u32[]{:S(2)}) %all-to-all-start.1) | async-done | bytes 65568 | tf_op jit(solution)/shard_map/all_to_all | solution.py:16
  98.2 11.1 %all-to-all-start.3 = ((f32[64,1,2048]{2,1,0:T(1,128)}), f32[64,1,2048]{2,1,0:T(1,128)S(1)}, u32[]{:S(2)}, u32[]{:S(2)}) async-start(f32[64,1,2048]{2,1,0:T(1,128)} %all_to_all.30), calls=%async_computation.3 | async-start | bytes 1048576 | tf_op jit(solution)/shard_map/all_to_all | solution.py:64
  109.3 0.6 broadcast.79
  109.9 0.9 reduce.1
  110.9 0.8 gather_fusion
  111.7 26.6 %all-to-all-done.3 = f32[64,1,2048]{2,1,0:T(1,128)S(1)} async-done(((f32[64,1,2048]{2,1,0:T(1,128)}), f32[64,1,2048]{2,1,0:T(1,128)S(1)}, u32[]{:S(2)}, u32[]{:S(2)}) %all-to-all-start.3) | async-done | bytes 524320 | tf_op jit(solution)/shard_map/all_to_all | solution.py:64
  138.3 0.3 reduce_sum.38
  138.6 1.1 broadcast_in_dim.46
  139.7 8.9 %all-to-all-start.4 = ((f32[64,1,2048]{2,1,0:T(1,128)}), f32[64,1,2048]{2,1,0:T(1,128)S(1)}, u32[]{:S(2)}, u32[]{:S(2)}) async-start(f32[64,1,2048]{2,1,0:T(1,128)} %broadcast_in_dim.46), calls=%async_computation.4 | async-start | bytes 1048576 | tf_op jit(solution)/shard_map/all_to_all | solution.py:16
  148.6 0.2 fusion.15
  149.2 0.2 fusion.7
  149.8 0.2 fusion.9
  150.5 27.4 %all-to-all-done.4 = f32[64,1,2048]{2,1,0:T(1,128)S(1)} async-done(((f32[64,1,2048]{2,1,0:T(1,128)}), f32[64,1,2048]{2,1,0:T(1,128)S(1)}, u32[]{:S(2)}, u32[]{:S(2)}) %all-to-all-start.4) | async-done | bytes 524320 | tf_op jit(solution)/shard_map/all_to_all | solution.py:16
  178.2 8.8 %all_to_all.44 = f32[2,64,2048]{2,1,0:T(8,128)S(1)} all-to-all(f32[2,64,2048]{2,1,0:T(8,128)S(1)} %broadcast_in_dim.47), channel_id=1, replica_groups=mesh['row'=4,'col'=16,'dep_0'=4,'dep_1'=2] {'dep_1'}, dimensions={0} | all-to-all | bytes 2097152 | tf_op jit(solution)/shard_map/all_to_all | solution.py:16
  187.0 1.0 fusion.25
  188.1 0.5 copy-done.1
  188.5 3.5 %convolution_subtract_fusion.1 = f32[4096,128]{1,0:T(8,128)S(1)} fusion(f32[4096,128]{1,0:T(8,128)S(1)} %copy-done.1, f32[64,4096]{1,0:T(8,128)S(1)} %fusion.25, f32[4,64,128]{2,1,0:T(8,128)S(1)} %bitcast.55, s32[]{:T(128)S(6)} %select_n.43), kind=kOutput, calls=%fused_computation.2 | convolution fusion | flops 403177472 | bytes 5275652 | tf_op jit(solution)/shard_map/dot_general | solution.py:75
  192.0 1.4 fusion.26
  193.4 7.2 %all_to_all.45 = f32[4,64,128]{2,1,0:T(8,128)S(1)} all-to-all(f32[4,64,128]{2,1,0:T(8,128)S(1)} %broadcast_in_dim.48), channel_id=1, replica_groups=mesh['row'=4,'col'=16,'dep_0'=4,'dep_1'=2] {'row'}, dimensions={0} | all-to-all | bytes 262144 | tf_op jit(solution)/shard_map/all_to_all | solution.py:16
  200.7 0.2 fusion.27
  200.9 4.8 %convolution_subtract_fusion = f32[4096,128]{1,0:T(8,128)} fusion(f32[4096,128]{1,0:T(8,128)S(1)} %convolution_subtract_fusion.1, f32[64,4096]{1,0:T(8,128)S(1)} %select_select_fusion, f32[64,128]{1,0:T(8,128)S(1)} %fusion.27), kind=kOutput, calls=%fused_computation.1 | convolution fusion | flops 403177472 | bytes 5275648 | tf_op jit(solution)/shard_map/dot_general | solution.py:75
  (26 shorter events, 1.9 us)
Async XLA Ops:
  1.9 60.6 %all-to-all-start = ((f32[16,64,256]{2,1,0:T(8,128)}), f32[16,64,256]{2,1,0:T(8,128)S(1)}, u32[]{:S(2)}, u32[]{:S(2)}) async-start(f32[16,64,256]{2,1,0:T(8,128)} %broadcast_in_dim.40), calls=%async_computation | async-start | bytes 2097152 | tf_op jit(solution)/shard_map/all_to_all | solution.py:16
  64.6 10.1 %copy-start = (f32[4096,128]{1,0:T(8,128)S(1)}, f32[4096,128]{1,0:T(8,128)}, u32[]{:S(2)}) copy-start(f32[4096,128]{1,0:T(8,128)} %param.2) | copy-start | bytes 6291460
  90.2 8.0 %all-to-all-start.1 = ((f32[4,1,4096]{2,1,0:T(1,128)}), f32[4,1,4096]{2,1,0:T(1,128)S(1)}, u32[]{:S(2)}, u32[]{:S(2)}) async-start(f32[4,1,4096]{2,1,0:T(1,128)} %reshape.81), calls=%async_computation.1 | async-start | bytes 131072 | tf_op jit(solution)/shard_map/all_to_all | solution.py:16
  98.2 40.1 %all-to-all-start.3 = ((f32[64,1,2048]{2,1,0:T(1,128)}), f32[64,1,2048]{2,1,0:T(1,128)S(1)}, u32[]{:S(2)}, u32[]{:S(2)}) async-start(f32[64,1,2048]{2,1,0:T(1,128)} %all_to_all.30), calls=%async_computation.3 | async-start | bytes 1048576 | tf_op jit(solution)/shard_map/all_to_all | solution.py:64
  139.7 38.2 %all-to-all-start.4 = ((f32[64,1,2048]{2,1,0:T(1,128)}), f32[64,1,2048]{2,1,0:T(1,128)S(1)}, u32[]{:S(2)}, u32[]{:S(2)}) async-start(f32[64,1,2048]{2,1,0:T(1,128)} %broadcast_in_dim.46), calls=%async_computation.4 | async-start | bytes 1048576 | tf_op jit(solution)/shard_map/all_to_all | solution.py:16
  186.9 1.6 copy-start.1
where the time goes:
time: 206 us
  waiting for transfers between devices  102 us (50%)
  starting transfers between devices  39.3 us (19%)
  blocking collectives  38.9 us (19%)
  matrix products  16.3 us (8%)
  local copies, waits for them, and re-layouts  7.34 us (4%)
    all_to_all x3, waiting for transfers between devices, sent_to_all(): return lax.all_to_all(copies, axis, split_axis=0, concat_axis=0, tiled=True)  75.4 us
    all_to_all x3, starting transfers between devices, sent_to_all(): return lax.all_to_all(copies, axis, split_axis=0, concat_axis=0, tiled=True)  28.1 us
    all_to_all x1, waiting for transfers between devices, sum_in_two_steps(): return jnp.sum(lax.all_to_all(own, far, 0, 0, tiled=True), axis=0)  26.6 us
    all_to_all x2, blocking collectives, sent_to_all(): return lax.all_to_all(copies, axis, split_axis=0, concat_axis=0, tiled=True)  16 us
    dot_general x7, matrix products, contract(): return lax.dot_general(left, right, (dims, ((), ())), precision=highest)  14.6 us
    all_to_all x1, blocking collectives, sent_and_summed(): lax.all_to_all(cut_along(array, dim, devices), axis, 0, 0, tiled=True)  13.2 us
    all_to_all x1, starting transfers between devices, sum_in_two_steps(): return jnp.sum(lax.all_to_all(own, far, 0, 0, tiled=True), axis=0)  11.1 us
    all_gather x1, blocking collectives, from_root(): lax.all_gather(array, axis)  9.76 us
  transfers between devices with their start and end apart: 4, of which 4 were waited for; matrix products, arithmetic and copies ran while one was open for 2% of the time, Pallas kernels for 0%

commit v1 on v0

v1 whole, which is shorter than its diff:
```python
import jax
import jax.numpy as jnp
from jax import lax
from jax.experimental import pallas as pl
from jax.experimental.pallas import tpu as pltpu
from jax.sharding import Mesh
from jax.sharding import PartitionSpec as P

AXES = ("row", "zh", "zl", "x", "core")
COLUMNS = ("zh", "zl", "x", "core")
PLANE = ("zl", "x")
LANES = 128
WIDTH = 64

highest = lax.Precision.HIGHEST
NN = ((1,), (0,))
NT = ((1,), (1,))
TN = ((0,), (0,))


def exact(left, right, dims):
    return lax.dot_general(
        left, right, (dims, ((), ())), precision=highest, preferred_element_type=jnp.float32
    )


def split(array):
    high = array.astype(jnp.bfloat16)
    return high, (array - high.astype(jnp.float32)).astype(jnp.bfloat16)


def three_pass(left, right, dims):
    def dot(a, b):
        return lax.dot_general(a, b, (dims, ((), ())), preferred_element_type=jnp.float32)

    return dot(left[0], right[0]) + (dot(left[0], right[1]) + dot(left[1], right[0]))


def swapped(array, axes):
    return lax.all_to_all(array, axes, 0, 0, tiled=True)


def shared(array, axes):
    return swapped(jnp.broadcast_to(array, (lax.axis_size(axes), *array.shape)), axes)


def mask_vectors(values, first_row):
    panel_width, row_count = values.shape
    positions = first_row + lax.iota(jnp.int32, row_count)[None, :]
    reflector = lax.iota(jnp.int32, panel_width)[:, None]
    filler = jnp.where(positions == reflector + 1, 1.0, 0.0).astype(values.dtype)
    return jnp.where(positions > reflector + 1, values, filler)


def column_routes():
    turn = {0: 2, 1: 1, 2: 0, 3: 3}
    pairs = []
    for y in range(4):
        for z in range(16):
            for x in range(4):
                for core in range(2):
                    to_x, to_z = z % 4, y * 4 + z // 4
                    to_y = (y + turn[(x - to_x) % 4]) % 4
                    here = ((y * 16 + z) * 4 + x) * 2 + core
                    pairs.append((here, ((to_y * 16 + to_z) * 4 + to_x) * 2 + core))
    return pairs


def value_kernel(columns_ref, matrix_ref, out_ref):
    left = split(columns_ref[...])
    for k in range(8):
        right = split(matrix_ref[k * LANES : (k + 1) * LANES, :])
        out_ref[k] = three_pass(left, right, NT)


def partial_value(columns, matrix):
    return pl.pallas_call(
        value_kernel,
        grid=(4,),
        in_specs=[
            pl.BlockSpec((WIDTH, LANES), lambda i: (0, 0)),
            pl.BlockSpec((8 * LANES, LANES), lambda i: (i, 0)),
        ],
        out_specs=pl.BlockSpec((8, WIDTH, LANES), lambda i: (i, 0, 0)),
        out_shape=jax.ShapeDtypeStruct((32, WIDTH, LANES), jnp.float32),
        name="value",
    )(columns, matrix)


def reflector_block(joined_ref, step, k):
    start = pl.multiple_of(WIDTH + step * 16 + (k % 2) * 8, 8)
    return joined_ref[:, k // 2, :, pl.ds(start, 8), :].reshape(WIDTH, LANES)


def value_block(joined_ref, step, k):
    return joined_ref[step // 2, (step % 2) * 2 + k // 4, k % 4, :WIDTH, :]


def terms_kernel(joined_ref, matrix_ref, out_ref):
    step = pl.program_id(0)

    @pl.when(step == 0)
    def _():
        out_ref[...] = jnp.zeros_like(out_ref)

    plain = jnp.zeros((WIDTH, LANES), jnp.float32)
    inner = jnp.zeros((WIDTH, LANES), jnp.float32)
    for k in range(8):
        rows = reflector_block(joined_ref, step, k)
        left = split(rows)
        plain += three_pass(left, split(matrix_ref[k * LANES : (k + 1) * LANES, :]), NN)
        other = jnp.concatenate([value_block(joined_ref, step, k), rows], axis=0)
        inner += exact(rows, other, NT)
    out_ref[:, :LANES] += plain
    out_ref[:, LANES:] += inner


def left_parts(joined, matrix):
    return pl.pallas_call(
        terms_kernel,
        grid=(4,),
        in_specs=[
            pl.BlockSpec(joined.shape, lambda i: (0, 0, 0, 0, 0)),
            pl.BlockSpec((8 * LANES, LANES), lambda i: (i, 0)),
        ],
        out_specs=pl.BlockSpec((WIDTH, 2 * LANES), lambda i: (0, 0)),
        out_shape=jax.ShapeDtypeStruct((WIDTH, 2 * LANES), jnp.float32),
        name="terms",
    )(joined, matrix)


def make_factor(gram):
    size_b = gram.shape[0]
    down = lax.broadcasted_iota(jnp.int32, (size_b, size_b), 0)
    across = lax.broadcasted_iota(jnp.int32, (size_b, size_b), 1)
    identity = jnp.where(down == across, 1.0, 0.0)
    half = 0.5 * jnp.where(down == across, gram, 0.0)
    half_down = jnp.sum(half, axis=1, keepdims=True)
    half_across = jnp.sum(half, axis=0, keepdims=True)
    scaled = jnp.where(across > down, gram, 0.0) / half_down
    inverse = identity - scaled
    powered = scaled
    for level in range((size_b - 1).bit_length() - 1):
        powered = exact(powered, powered, NN)
        inverse = exact(inverse, identity + powered, NN)
    return inverse / half_across


def last_kernel(parts_ref, columns_ref, joined_ref, matrix_ref, out_ref, right_ref):
    step = pl.program_id(0)

    @pl.when(step == 0)
    def _():
        total = (parts_ref[0] + parts_ref[1]) + (parts_ref[2] + parts_ref[3])
        factor = make_factor(total[:, LANES + WIDTH :])
        right = exact(factor, columns_ref[...], NN)
        left = total[:, :LANES] - exact(total[:, LANES : LANES + WIDTH], right, NN)
        right_ref[:WIDTH, :] = right
        right_ref[WIDTH:, :] = exact(factor, left, TN)

    right = split(right_ref[...])
    for k in range(8):
        left = jnp.concatenate(
            [value_block(joined_ref, step, k), reflector_block(joined_ref, step, k)], axis=0
        )
        change = three_pass(split(left), right, TN)
        span = slice(k * LANES, (k + 1) * LANES)
        out_ref[span, :] = matrix_ref[span, :] - change


def last_step(parts, columns, joined, matrix):
    return pl.pallas_call(
        last_kernel,
        grid=(4,),
        in_specs=[
            pl.BlockSpec(parts.shape, lambda i: (0, 0, 0)),
            pl.BlockSpec((WIDTH, LANES), lambda i: (0, 0)),
            pl.BlockSpec(joined.shape, lambda i: (0, 0, 0, 0, 0)),
            pl.BlockSpec((8 * LANES, LANES), lambda i: (i, 0)),
        ],
        out_specs=pl.BlockSpec((8 * LANES, LANES), lambda i: (i, 0)),
        out_shape=jax.ShapeDtypeStruct(matrix.shape, jnp.float32),
        scratch_shapes=[pltpu.VMEM((2 * WIDTH, LANES), jnp.float32)],
        name="last",
    )(parts, columns, joined, matrix)


def on_device(matrix, vectors):
    width, piece = vectors.shape
    core, x = lax.axis_index("core"), lax.axis_index("x")
    masked = mask_vectors(vectors, lax.axis_index(("row", "zh", "zl")) * piece)
    half = lax.dynamic_slice_in_dim(masked, core * LANES, LANES, 1)
    columns = lax.ppermute(half, AXES, column_routes())
    lines = lax.dynamic_slice_in_dim(masked, (core * 4 + x) * 8, 8, 0)
    lines = lines.reshape(8, 2, LANES).swapaxes(0, 1).reshape(16, LANES)

    values = partial_value(columns, matrix)
    values = swapped(values.reshape(2, 16, WIDTH, LANES), "core").sum(axis=0)
    values = swapped(values, PLANE).sum(axis=0)
    far = shared(jnp.concatenate([values, lines], axis=0), "zh")
    summed = far[:, :WIDTH].sum(axis=0)
    own = jnp.concatenate([summed, far[:, WIDTH:].reshape(WIDTH, LANES)], axis=0)
    joined = shared(shared(own, PLANE), "core").reshape(2, 4, 4, 2 * WIDTH, LANES)

    parts = shared(left_parts(joined, matrix), "row")
    return last_step(parts, columns, joined, matrix)


def solution(mesh):
    torus = Mesh(mesh.devices.reshape(4, 4, 4, 4, 2), AXES)
    placed = (P("row", COLUMNS), P(None, ("row", "zh", "zl")))
    return jax.shard_map(
        on_device, mesh=torus, in_specs=placed, out_specs=P("row", COLUMNS), check_vma=False
    )
```

time: 206 us -> 143 us (0.69)
  waiting for transfers between devices: 102 us -> 15.2 us
  blocking collectives: 38.9 us -> 87 us
  starting transfers between devices: 39.3 us -> 17.1 us
  Pallas kernels: 0 us -> 19.1 us
  matrix products: 16.3 us -> 0 us
  local copies, waits for them, and re-layouts: 7.34 us -> 1.82 us
    all_to_all x4 -> x1, waiting for transfers between devices: 102 us -> 14.1 us  [swapped(): return lax.all_to_all(array, axes, 0, 0, tiled=True)]
    all_to_all x3 -> x5, blocking collectives: 29.2 us -> 87 us  [swapped(): return lax.all_to_all(array, axes, 0, 0, tiled=True)]
    all_to_all x4 -> x1, starting transfers between devices: 39.3 us -> 11.4 us  [swapped(): return lax.all_to_all(array, axes, 0, 0, tiled=True)]
    pallas_call x0 -> x3, Pallas kernels: none -> 19.1 us  [the longest x1 7.2 us: left_parts(): pl.pallas_call(terms_kernel, grid=(4,), in_specs=[pl.BlockSpec(joined.sha...]
    dot_general x17 -> x0, matrix products: 16.3 us -> none  [the longest x7 14.6 us: contract(): return lax.dot_general(left, right, (dims, ((), ())), precision=highest)]
    all_gather x1 -> x0, blocking collectives: 9.76 us -> none  [from_root(): lax.all_gather(array, axis)]
    ppermute x0 -> x1, starting transfers between devices: none -> 5.65 us  [on_device(): columns = lax.ppermute(half, AXES, column_routes())]
  transfers between devices with their start and end apart: 4 -> 2, of which waited for: 4 -> 2; matrix products, arithmetic and copies ran while one was open for 2% -> 0% of each run, Pallas kernels for 0% -> 0%
where the time goes in v1:
time: 143 us; the launch traced here: 142 us
  blocking collectives  87 us (61%)
  Pallas kernels  19.1 us (13%)
  starting transfers between devices  17.1 us (12%)
  waiting for transfers between devices  15.2 us (11%)
  other arithmetic  1.88 us (1%)
  local copies, waits for them, and re-layouts  1.82 us (1%)
    all_to_all x5, blocking collectives, swapped(): return lax.all_to_all(array, axes, 0, 0, tiled=True)  87 us
    all_to_all x1, waiting for transfers between devices, swapped(): return lax.all_to_all(array, axes, 0, 0, tiled=True)  14.1 us
    all_to_all x1, starting transfers between devices, swapped(): return lax.all_to_all(array, axes, 0, 0, tiled=True)  11.4 us
    pallas_call x1, Pallas kernels, left_parts(): pl.pallas_call(terms_kernel, grid=(4,), in_specs=[pl.BlockSpec(joined.sha...  7.2 us
    pallas_call x1, Pallas kernels, last_step(): pl.pallas_call(last_kernel, grid=(4,), in_specs=[pl.BlockSpec(parts.shape...  7.12 us
    ppermute x1, starting transfers between devices, on_device(): columns = lax.ppermute(half, AXES, column_routes())  5.65 us
    pallas_call x1, Pallas kernels, partial_value(): pl.pallas_call(value_kernel, grid=(4,), in_specs=[pl.BlockSpec((WIDTH, LA...  4.83 us
  transfers between devices with their start and end apart: 2, of which 2 were waited for; matrix products, arithmetic and copies ran while one was open for 0% of the time, Pallas kernels for 0%

profile of v1, /device:TPU:1, one launch (start us, length us, event | category | flops | bytes accessed | tf_op | source)
XLA Modules:
  0.0 142.2 jit_solution(11923429949237250568)
XLA Ops:
  0.0 0.9 select_select_fusion
  1.0 5.7 %collective-permute-start = (f32[64,128]{1,0:T(8,128)S(1)}, f32[64,128]{1,0:T(8,128)S(1)}, u32[]{:S(2)}, u32[]{:S(2)}) collective-permute-start(f32[64,128]{1,0:T(8,128)S(1)} %constant_dynamic-slice_fusion), channel_id=1, source_target_pairs={{0,256},{1,257},{2,128},{3,129},{4,0},{5,1},{6,384},{7,385},{8,386... | collective-permute-start | bytes 98312 | tf_op jit(solution)/shard_map/ppermute | solution.py:193
  6.6 1.1 collective-permute-done.columns_ref
  7.7 0.0 copy-start
  7.7 0.6 copy-done
  8.3 4.8 %value.1 = f32[32,64,128]{2,1,0:T(8,128)} custom-call(f32[64,128]{1,0:T(8,128)} %copy-done, f32[4096,128]{1,0:T(8,128)} %matrix_ref.5), custom_call_target="tpu_custom_call" | custom-call | tf_op jit(solution)/shard_map/value/pallas_call | solution.py:77
  13.2 12.7 %all_to_all.30 = f32[2,16,64,128]{3,2,1,0:T(8,128)S(1)} all-to-all(f32[2,16,64,128]{3,2,1,0:T(8,128)} %bitcast.11), channel_id=1, replica_groups=mesh['row'=4,'zh'=4,'zl'=4,'x'=4,'core'=2] {'core'}, dimensions={0} | all-to-all | bytes 2097152 | tf_op jit(solution)/shard_map/all_to_all | solution.py:40
  25.9 0.9 reduce_sum.27
  26.8 11.4 %all-to-all-start.1 = ((f32[16,64,128]{2,1,0:T(8,128)}), f32[16,64,128]{2,1,0:T(8,128)S(1)}, u32[]{:S(2)}, u32[]{:S(2)}) async-start(f32[16,64,128]{2,1,0:T(8,128)} %reduce_sum.27), calls=%async_computation.1 | async-start | bytes 1048576 | tf_op jit(solution)/shard_map/all_to_all | solution.py:40
  38.2 14.1 %all-to-all-done.1 = f32[16,64,128]{2,1,0:T(8,128)S(1)} async-done(((f32[16,64,128]{2,1,0:T(8,128)}), f32[16,64,128]{2,1,0:T(8,128)S(1)}, u32[]{:S(2)}, u32[]{:S(2)}) %all-to-all-start.1) | async-done | bytes 524320 | tf_op jit(solution)/shard_map/all_to_all | solution.py:40
  52.4 25.4 %all_to_all.31 = f32[4,80,128]{2,1,0:T(8,128)S(1)} all-to-all(f32[4,80,128]{2,1,0:T(8,128)S(1)} %broadcast_in_dim.24), channel_id=1, replica_groups=mesh['row'=4,'zh'=4,'zl'=4,'x'=4,'core'=2] {'zh'}, dimensions={0} | all-to-all | bytes 327680 | tf_op jit(solution)/shard_map/all_to_all | solution.py:40
  77.8 0.1 broadcast_in_dim.25
  78.0 29.5 %all_to_all.32 = f32[16,128,128]{2,1,0:T(8,128)S(1)} all-to-all(f32[16,128,128]{2,1,0:T(8,128)S(1)} %broadcast_in_dim.25), channel_id=1, replica_groups=mesh['row'=4,'zh'=4,'zl'=4,'x'=4,'core'=2] {'zl','x'}, dimensions={0} | all-to-all | bytes 2097152 | tf_op jit(solution)/shard_map/all_to_all | solution.py:40
  107.4 0.2 broadcast_in_dim.26
  107.7 9.5 %all_to_all.33 = f32[2,16,128,128]{3,2,1,0:T(8,128)} all-to-all(f32[2,16,128,128]{3,2,1,0:T(8,128)S(1)} %broadcast_in_dim.26), channel_id=1, replica_groups=mesh['row'=4,'zh'=4,'zl'=4,'x'=4,'core'=2] {'core'}, dimensions={0} | all-to-all | bytes 4194304 | tf_op jit(solution)/shard_map/all_to_all | solution.py:40
  117.2 7.2 %terms.1 = f32[64,256]{1,0:T(8,128)} custom-call(f32[2,4,4,128,128]{4,3,2,1,0:T(8,128)} %bitcast.9, f32[4096,128]{1,0:T(8,128)} %matrix_ref.5), custom_call_target="tpu_custom_call" | custom-call | tf_op jit(solution)/shard_map/terms/pallas_call | solution.py:119
  124.4 0.9 broadcast_in_dim.27
  125.2 9.9 %all_to_all.34.parts_ref = f32[4,64,256]{2,1,0:T(8,128)} all-to-all(f32[4,64,256]{2,1,0:T(8,128)S(1)} %broadcast_in_dim.27), channel_id=1, replica_groups=mesh['row'=4,'zh'=4,'zl'=4,'x'=4,'core'=2] {'row'}, dimensions={0} | all-to-all | bytes 524288 | tf_op jit(solution)/shard_map/all_to_all | solution.py:40
  135.1 7.1 %last.1 = f32[4096,128]{1,0:T(8,128)} custom-call(f32[4,64,256]{2,1,0:T(8,128)} %all_to_all.34.parts_ref, f32[64,128]{1,0:T(8,128)} %copy-done, f32[2,4,4,128,128]{4,3,2,1,0:T(8,128)} %bitcast.10, f32[4096,128]{1,0:T(8,128)} %matrix_ref.5), custom_call_target="tpu_custom_call" | custom-call | tf_op jit(solution)/shard_map/last/pallas_call | solution.py:172
  (10 shorter events, 0.1 us)
Async XLA Ops:
  1.0 6.8 %collective-permute-start = (f32[64,128]{1,0:T(8,128)S(1)}, f32[64,128]{1,0:T(8,128)S(1)}, u32[]{:S(2)}, u32[]{:S(2)}) collective-permute-start(f32[64,128]{1,0:T(8,128)S(1)} %constant_dynamic-slice_fusion), channel_id=1, source_target_pairs={{0,256},{1,257},{2,128},{3,129},{4,0},{5,1},{6,384},{7,385},{8,386... | collective-permute-start | bytes 98312 | tf_op jit(solution)/shard_map/ppermute | solution.py:193
  7.7 0.6 copy-start
  26.8 25.5 %all-to-all-start.1 = ((f32[16,64,128]{2,1,0:T(8,128)}), f32[16,64,128]{2,1,0:T(8,128)S(1)}, u32[]{:S(2)}, u32[]{:S(2)}) async-start(f32[16,64,128]{2,1,0:T(8,128)} %reduce_sum.27), calls=%async_computation.1 | async-start | bytes 1048576 | tf_op jit(solution)/shard_map/all_to_all | solution.py:40

commit v2 on v1

v2 whole, which is shorter than its diff:
```python
import jax
import jax.numpy as jnp
from jax import lax
from jax.experimental import pallas as pl
from jax.experimental.pallas import tpu as pltpu
from jax.sharding import Mesh
from jax.sharding import PartitionSpec as P

AXES = ("row", "zh", "zl", "x", "core")
COLUMNS = ("zh", "zl", "x", "core")
PLANE = ("zl", "x")
LANES = 128
WIDTH = 64
ROOM = pltpu.CompilerParams(vmem_limit_bytes=16 * 1024 * 1024)

highest = lax.Precision.HIGHEST
NN = ((1,), (0,))
NT = ((1,), (1,))
TN = ((0,), (0,))


def exact(left, right, dims):
    return lax.dot_general(
        left, right, (dims, ((), ())), precision=highest, preferred_element_type=jnp.float32
    )


def split(array):
    high = array.astype(jnp.bfloat16)
    return high, (array - high.astype(jnp.float32)).astype(jnp.bfloat16)


def dot(left, right, dims):
    return lax.dot_general(left, right, (dims, ((), ())), preferred_element_type=jnp.float32)


def swapped(array, axes):
    return lax.all_to_all(array, axes, 0, 0, tiled=True)


def shared(array, axes):
    return swapped(jnp.broadcast_to(array, (lax.axis_size(axes), *array.shape)), axes)


def mask_vectors(values, first_row):
    panel_width, row_count = values.shape
    positions = first_row + lax.iota(jnp.int32, row_count)[None, :]
    reflector = lax.iota(jnp.int32, panel_width)[:, None]
    filler = jnp.where(positions == reflector + 1, 1.0, 0.0).astype(values.dtype)
    return jnp.where(positions > reflector + 1, values, filler)


def column_routes():
    turn = {0: 2, 1: 1, 2: 0, 3: 3}
    pairs = []
    for y in range(4):
        for z in range(16):
            for x in range(4):
                for core in range(2):
                    to_x, to_z = z % 4, y * 4 + z // 4
                    to_y = (y + turn[(x - to_x) % 4]) % 4
                    here = ((y * 16 + z) * 4 + x) * 2 + core
                    pairs.append((here, ((to_y * 16 + to_z) * 4 + to_x) * 2 + core))
    return pairs


def doubled(array):
    blank = jnp.zeros_like(array)
    return jnp.concatenate(
        [jnp.concatenate([array, blank], axis=1), jnp.concatenate([blank, array], axis=1)], axis=0
    )


def local(array):
    return pltpu.with_memory_space_constraint(array, pltpu.VMEM)


def in_vmem(count):
    return [pl.BlockSpec(memory_space=pltpu.VMEM)] * count


def value_kernel(columns_ref, matrix_ref, out_ref):
    high, low = split(doubled(columns_ref[...].T))
    right = jnp.concatenate([high, low], axis=1)
    for unit in range(16):
        first = matrix_ref[2 * unit * LANES : (2 * unit + 1) * LANES, :]
        second = matrix_ref[(2 * unit + 1) * LANES : (2 * unit + 2) * LANES, :]
        high, low = split(jnp.concatenate([first, second], axis=1))
        both = dot(high, right, NN) + dot(low, right, NN)
        total = both[:, :LANES] + both[:, LANES:]
        out_ref[2 * unit : 2 * unit + 2] = total.reshape(2, WIDTH, LANES)


def partial_value(columns, matrix):
    return pl.pallas_call(
        value_kernel,
        in_specs=in_vmem(2),
        out_specs=in_vmem(1)[0],
        out_shape=pltpu.VMEM((32, WIDTH, LANES), jnp.float32),
        compiler_params=ROOM,
        name="value",
    )(columns, matrix)


def reflector_block(joined_ref, unit, half):
    zh, zl = divmod(unit, 4)
    start = WIDTH + zh * 16 + half * 8
    return joined_ref[:, zl, :, start : start + 8, :].reshape(WIDTH, LANES)


def value_unit(joined_ref, unit):
    piece = 2 * unit
    core, zl, x = piece // 16, piece // 4 % 4, piece % 4
    return joined_ref[core, zl, x : x + 2, :WIDTH, :].reshape(2 * WIDTH, LANES)


def in_three(array):
    high, low = split(array)
    rest = array - high.astype(jnp.float32) - low.astype(jnp.float32)
    return jnp.concatenate([high, low, rest.astype(jnp.bfloat16)], axis=0)


def terms_kernel(joined_ref, matrix_ref, out_ref):
    plain = jnp.zeros((2 * WIDTH, 2 * LANES), jnp.float32)
    cross = jnp.zeros((4 * WIDTH, 2 * LANES), jnp.float32)
    gram = jnp.zeros((3 * WIDTH, 3 * WIDTH), jnp.float32)
    for unit in range(16):
        rows = [reflector_block(joined_ref, unit, half) for half in range(2)]
        rows = in_three(jnp.concatenate(rows, axis=1))
        span = slice(2 * unit * LANES, 2 * (unit + 1) * LANES)
        right = jnp.concatenate(split(matrix_ref[span, :]), axis=1)
        plain += dot(rows[: 2 * WIDTH], right, NN)
        right = jnp.concatenate(split(value_unit(joined_ref, unit)), axis=1)
        both = [rows[: 2 * WIDTH, :LANES], rows[: 2 * WIDTH, LANES:]]
        cross += dot(jnp.concatenate(both, axis=0), right, NN)
        gram += dot(rows, rows, NT)
    plain = plain[:WIDTH] + plain[WIDTH:]
    plain = plain[:, :LANES] + plain[:, LANES:]
    cross = cross[:, :LANES] + cross[:, LANES:]
    first = cross[:WIDTH] + cross[WIDTH : 2 * WIDTH]
    second = cross[2 * WIDTH : 3 * WIDTH] + cross[3 * WIDTH :]
    cross = first[:, :WIDTH] + second[:, WIDTH:]
    gram = gram[:WIDTH] + (gram[WIDTH : 2 * WIDTH] + gram[2 * WIDTH :])
    gram = gram[:, :WIDTH] + (gram[:, WIDTH : 2 * WIDTH] + gram[:, 2 * WIDTH :])
    joined = jnp.concatenate([plain, cross, gram], axis=1)
    for y in range(4):
        out_ref[y] = joined


def left_parts(joined, matrix):
    return pl.pallas_call(
        terms_kernel,
        in_specs=in_vmem(2),
        out_specs=in_vmem(1)[0],
        out_shape=pltpu.VMEM((4, WIDTH, 2 * LANES), jnp.float32),
        compiler_params=ROOM,
        name="terms",
    )(joined, matrix)


def make_factor(gram):
    size_b = gram.shape[0]
    down = lax.broadcasted_iota(jnp.int32, (size_b, size_b), 0)
    across = lax.broadcasted_iota(jnp.int32, (size_b, size_b), 1)
    identity = jnp.where(down == across, 1.0, 0.0)
    half = 0.5 * jnp.where(down == across, gram, 0.0)
    half_down = jnp.sum(half, axis=1, keepdims=True)
    half_across = jnp.sum(half, axis=0, keepdims=True)
    scaled = jnp.where(across > down, gram, 0.0) / half_down
    inverse = identity - scaled
    powered = scaled
    for level in range((size_b - 1).bit_length() - 1):
        powered = exact(powered, powered, NN)
        inverse = exact(inverse, identity + powered, NN)
    return inverse / half_across


def last_kernel(parts_ref, columns_ref, joined_ref, matrix_ref, out_ref, done_ref, sems):
    total = (parts_ref[0] + parts_ref[1]) + (parts_ref[2] + parts_ref[3])
    factor = make_factor(total[:, LANES + WIDTH :])
    right = exact(factor, columns_ref[...], NN)
    left = total[:, :LANES] - exact(total[:, LANES : LANES + WIDTH], right, NN)
    left = exact(factor, left, TN)
    high, low = split(jnp.concatenate([doubled(right), doubled(left)], axis=0))
    copies = []
    for unit in range(16):
        rows = [reflector_block(joined_ref, unit, half) for half in range(2)]
        rows = jnp.concatenate(rows, axis=0).T
        left = split(jnp.concatenate([value_unit(joined_ref, unit), rows], axis=1))
        change = dot(left[0], high, NN) + (dot(left[0], low, NN) + dot(left[1], high, NN))
        for half in range(2):
            start = (2 * unit + half) * LANES
            span = slice(start, start + LANES)
            done_ref[span, :] = matrix_ref[span, :] - change[:, half * LANES : (half + 1) * LANES]
        if unit % 4 == 3:
            part = pl.ds((unit - 3) * 2 * LANES, 8 * LANES)
            copy = pltpu.make_async_copy(done_ref.at[part], out_ref.at[part], sems.at[unit // 4])
            copy.start()
            copies.append(copy)
    for copy in copies:
        copy.wait()


def last_step(parts, columns, joined, matrix):
    return pl.pallas_call(
        last_kernel,
        in_specs=in_vmem(4),
        out_specs=pl.BlockSpec(memory_space=pl.ANY),
        out_shape=jax.ShapeDtypeStruct(matrix.shape, jnp.float32),
        scratch_shapes=[
            pltpu.VMEM(matrix.shape, jnp.float32),
            pltpu.SemaphoreType.DMA((4,)),
        ],
        compiler_params=ROOM,
        name="last",
    )(parts, columns, joined, matrix)


def on_device(matrix, vectors):
    width, piece = vectors.shape
    core, x = lax.axis_index("core"), lax.axis_index("x")
    masked = mask_vectors(vectors, lax.axis_index(("row", "zh", "zl")) * piece)
    half = lax.dynamic_slice_in_dim(masked, core * LANES, LANES, 1)
    columns = lax.ppermute(half, AXES, column_routes())
    lines = lax.dynamic_slice_in_dim(masked, (core * 4 + x) * 8, 8, 0)
    lines = lines.reshape(8, 2, LANES).swapaxes(0, 1).reshape(16, LANES)

    matrix, columns = local(matrix), local(columns)
    values = partial_value(columns, matrix)
    values = swapped(values.reshape(2, 16, WIDTH, LANES), "core").sum(axis=0)
    values = swapped(values, PLANE).sum(axis=0)
    far = shared(jnp.concatenate([values, lines], axis=0), "zh")
    summed = far[:, :WIDTH].sum(axis=0)
    own = jnp.concatenate([summed, far[:, WIDTH:].reshape(WIDTH, LANES)], axis=0)
    joined = shared(shared(own, PLANE), "core")
    joined = local(joined.reshape(2, 4, 4, 2 * WIDTH, LANES))

    parts = local(swapped(left_parts(joined, matrix), "row"))
    return last_step(parts, columns, joined, matrix)


def solution(mesh):
    torus = Mesh(mesh.devices.reshape(4, 4, 4, 4, 2), AXES)
    placed = (P("row", COLUMNS), P(None, ("row", "zh", "zl")))
    return jax.shard_map(
        on_device, mesh=torus, in_specs=placed, out_specs=P("row", COLUMNS), check_vma=False
    )
```

time: 143 us -> 128 us (0.90)
  Pallas kernels: 19.1 us -> 6.16 us
  blocking collectives: 87 us -> 85 us
    pallas_call x3, Pallas kernels: 19.1 us -> 6.16 us  [the longest x1 3.58 us: last_step(): pl.pallas_call(last_kernel, in_specs=in_vmem(4), out_specs=pl.BlockSpec(m...]
    all_to_all x5, blocking collectives: 87 us -> 85 us  [swapped(): return lax.all_to_all(array, axes, 0, 0, tiled=True)]
where the time goes in v2:
time: 128 us; the launch traced here: 127 us
  blocking collectives  85 us (66%)
  starting transfers between devices  17.1 us (13%)
  waiting for transfers between devices  15.2 us (12%)
  Pallas kernels  6.16 us (5%)
  local copies, waits for them, and re-layouts  1.96 us (2%)
  other arithmetic  1.88 us (1%)
    all_to_all x5, blocking collectives, swapped(): return lax.all_to_all(array, axes, 0, 0, tiled=True)  85 us
    all_to_all x1, waiting for transfers between devices, swapped(): return lax.all_to_all(array, axes, 0, 0, tiled=True)  14.1 us
    all_to_all x1, starting transfers between devices, swapped(): return lax.all_to_all(array, axes, 0, 0, tiled=True)  11.4 us
    ppermute x1, starting transfers between devices, on_device(): columns = lax.ppermute(half, AXES, column_routes())  5.65 us
    pallas_call x1, Pallas kernels, last_step(): pl.pallas_call(last_kernel, in_specs=in_vmem(4), out_specs=pl.BlockSpec(m...  3.58 us
  transfers between devices with their start and end apart: 2, of which 2 were waited for; matrix products, arithmetic and copies ran while one was open for 0% of the time, Pallas kernels for 0%

profile of v2, /device:TPU:1, one launch (start us, length us, event | category | flops | bytes accessed | tf_op | source)
XLA Modules:
  0.0 127.4 jit_solution(2782099930621469531)
XLA Ops:
  0.0 0.9 select_select_fusion
  1.0 5.7 %collective-permute-start = (f32[64,128]{1,0:T(8,128)S(1)}, f32[64,128]{1,0:T(8,128)S(1)}, u32[]{:S(2)}, u32[]{:S(2)}) collective-permute-start(f32[64,128]{1,0:T(8,128)S(1)} %constant_dynamic-slice_fusion), channel_id=1, source_target_pairs={{0,256},{1,257},{2,128},{3,129},{4,0},{5,1},{6,384},{7,385},{8,386... | collective-permute-start | bytes 98312 | tf_op jit(solution)/shard_map/ppermute | solution.py:224
  6.6 1.1 collective-permute-done.columns_ref
  7.7 0.0 copy-start
  7.7 1.6 %copy-done = f32[4096,128]{1,0:T(8,128)S(1)} copy-done((f32[4096,128]{1,0:T(8,128)S(1)}, f32[4096,128]{1,0:T(8,128)}, u32[]{:S(2)}) %copy-start) | copy-done | bytes 2097176
  9.3 0.9 value.1
  10.2 11.6 %all_to_all.30 = f32[2,16,64,128]{3,2,1,0:T(8,128)S(1)} all-to-all(f32[2,16,64,128]{3,2,1,0:T(8,128)S(1)} %bitcast.11), channel_id=1, replica_groups=mesh['row'=4,'zh'=4,'zl'=4,'x'=4,'core'=2] {'core'}, dimensions={0} | all-to-all | bytes 2097152 | tf_op jit(solution)/shard_map/all_to_all | solution.py:38
  21.8 0.9 reduce_sum.27
  22.7 11.4 %all-to-all-start.1 = ((f32[16,64,128]{2,1,0:T(8,128)}), f32[16,64,128]{2,1,0:T(8,128)S(1)}, u32[]{:S(2)}, u32[]{:S(2)}) async-start(f32[16,64,128]{2,1,0:T(8,128)} %reduce_sum.27), calls=%async_computation.1 | async-start | bytes 1048576 | tf_op jit(solution)/shard_map/all_to_all | solution.py:38
  34.1 14.1 %all-to-all-done.1 = f32[16,64,128]{2,1,0:T(8,128)S(1)} async-done(((f32[16,64,128]{2,1,0:T(8,128)}), f32[16,64,128]{2,1,0:T(8,128)S(1)}, u32[]{:S(2)}, u32[]{:S(2)}) %all-to-all-start.1) | async-done | bytes 524320 | tf_op jit(solution)/shard_map/all_to_all | solution.py:38
  48.3 25.4 %all_to_all.31 = f32[4,80,128]{2,1,0:T(8,128)S(1)} all-to-all(f32[4,80,128]{2,1,0:T(8,128)S(1)} %broadcast_in_dim.21), channel_id=1, replica_groups=mesh['row'=4,'zh'=4,'zl'=4,'x'=4,'core'=2] {'zh'}, dimensions={0} | all-to-all | bytes 327680 | tf_op jit(solution)/shard_map/all_to_all | solution.py:38
  73.8 0.1 broadcast_in_dim.22
  73.9 29.5 %all_to_all.32 = f32[16,128,128]{2,1,0:T(8,128)S(1)} all-to-all(f32[16,128,128]{2,1,0:T(8,128)S(1)} %broadcast_in_dim.22), channel_id=1, replica_groups=mesh['row'=4,'zh'=4,'zl'=4,'x'=4,'core'=2] {'zl','x'}, dimensions={0} | all-to-all | bytes 2097152 | tf_op jit(solution)/shard_map/all_to_all | solution.py:38
  103.4 0.2 broadcast_in_dim.23
  103.6 0.0 copy-start.1
  103.6 8.7 %all_to_all.33 = f32[2,16,128,128]{3,2,1,0:T(8,128)S(1)} all-to-all(f32[2,16,128,128]{3,2,1,0:T(8,128)S(1)} %broadcast_in_dim.23), channel_id=1, replica_groups=mesh['row'=4,'zh'=4,'zl'=4,'x'=4,'core'=2] {'core'}, dimensions={0} | all-to-all | bytes 4194304 | tf_op jit(solution)/shard_map/all_to_all | solution.py:38
  112.4 0.0 copy-done.1
  112.4 1.7 %terms.1 = f32[4,64,256]{2,1,0:T(8,128)S(1)} custom-call(f32[2,4,4,128,128]{4,3,2,1,0:T(8,128)S(1)} %bitcast.9, f32[4096,128]{1,0:T(8,128)S(1)} %copy-done.1), custom_call_target="tpu_custom_call" | custom-call | tf_op jit(solution)/shard_map/terms/pallas_call | solution.py:151
  114.1 9.8 %all_to_all.34.parts_ref = f32[4,64,256]{2,1,0:T(8,128)S(1)} all-to-all(f32[4,64,256]{2,1,0:T(8,128)S(1)} %terms.1), channel_id=1, replica_groups=mesh['row'=4,'zh'=4,'zl'=4,'x'=4,'core'=2] {'row'}, dimensions={0} | all-to-all | bytes 524288 | tf_op jit(solution)/shard_map/all_to_all | solution.py:38
  123.8 3.6 %last.1 = f32[4096,128]{1,0:T(8,128)} custom-call(f32[4,64,256]{2,1,0:T(8,128)S(1)} %all_to_all.34.parts_ref, f32[64,128]{1,0:T(8,128)S(1)} %collective-permute-done.columns_ref, f32[2,4,4,128,128]{4,3,2,1,0:T(8,128)S(1)} %bitcast.10, f32[4096,128]{1,0:T(8,128)S(1)} %copy-done.1), custom_call_target="tpu_custom_call" | custom-call | tf_op jit(solution)/shard_map/last/pallas_call | solution.py:205
  (10 shorter events, 0.1 us)
Async XLA Ops:
  1.0 6.8 %collective-permute-start = (f32[64,128]{1,0:T(8,128)S(1)}, f32[64,128]{1,0:T(8,128)S(1)}, u32[]{:S(2)}, u32[]{:S(2)}) collective-permute-start(f32[64,128]{1,0:T(8,128)S(1)} %constant_dynamic-slice_fusion), channel_id=1, source_target_pairs={{0,256},{1,257},{2,128},{3,129},{4,0},{5,1},{6,384},{7,385},{8,386... | collective-permute-start | bytes 98312 | tf_op jit(solution)/shard_map/ppermute | solution.py:224
  7.7 1.6 %copy-start = (f32[4096,128]{1,0:T(8,128)S(1)}, f32[4096,128]{1,0:T(8,128)}, u32[]{:S(2)}) copy-start(f32[4096,128]{1,0:T(8,128)} %matrix_ref.5) | copy-start | bytes 6291460
  22.7 25.5 %all-to-all-start.1 = ((f32[16,64,128]{2,1,0:T(8,128)}), f32[16,64,128]{2,1,0:T(8,128)S(1)}, u32[]{:S(2)}, u32[]{:S(2)}) async-start(f32[16,64,128]{2,1,0:T(8,128)} %reduce_sum.27), calls=%async_computation.1 | async-start | bytes 1048576 | tf_op jit(solution)/shard_map/all_to_all | solution.py:38
  103.6 8.8 %copy-start.1 = (f32[4096,128]{1,0:T(8,128)S(1)}, f32[4096,128]{1,0:T(8,128)}, u32[]{:S(2)}) copy-start(f32[4096,128]{1,0:T(8,128)} %matrix_ref.5) | copy-start | bytes 6291460

commit v3 on v2

--- a/solution.py
+++ b/solution.py
@@ -77,6 +77,39 @@
 
 def in_vmem(count):
     return [pl.BlockSpec(memory_space=pltpu.VMEM)] * count
+
+
+def staging_kernel(matrix_ref, out_ref, sem):
+    copy = pltpu.make_async_copy(matrix_ref, out_ref, sem)
+    copy.start()
+    copy.wait()
+
+
+def staged(matrix):
+    return pl.pallas_call(
+        staging_kernel,
+        in_specs=[pl.BlockSpec(memory_space=pltpu.HBM)],
+        out_specs=in_vmem(1)[0],
+        out_shape=pltpu.VMEM(matrix.shape, jnp.float32),
+        scratch_shapes=[pltpu.SemaphoreType.DMA],
+        compiler_params=ROOM,
+        name="staging",
+    )(pltpu.with_memory_space_constraint(matrix, pltpu.HBM))
+
+
+def pair_kernel(pair_ref, out_ref):
+    out_ref[...] = pair_ref[0] + pair_ref[1]
+
+
+def pair_summed(pair):
+    return pl.pallas_call(
+        pair_kernel,
+        in_specs=in_vmem(1),
+        out_specs=in_vmem(1)[0],
+        out_shape=pltpu.VMEM(pair.shape[1:], jnp.float32),
+        compiler_params=ROOM,
+        name="pair",
+    )(local(pair))
 
 
 def value_kernel(columns_ref, matrix_ref, out_ref):
@@ -225,9 +258,10 @@
     lines = lax.dynamic_slice_in_dim(masked, (core * 4 + x) * 8, 8, 0)
     lines = lines.reshape(8, 2, LANES).swapaxes(0, 1).reshape(16, LANES)
 
-    matrix, columns = local(matrix), local(columns)
+    matrix, columns = staged(matrix), local(columns)
     values = partial_value(columns, matrix)
-    values = swapped(values.reshape(2, 16, WIDTH, LANES), "core").sum(axis=0)
+    values = pair_summed(swapped(values.reshape(2, 16, WIDTH, LANES), "core"))
+    values, lines = lax.optimization_barrier((values, lines))
     values = swapped(values, PLANE).sum(axis=0)
     far = shared(jnp.concatenate([values, lines], axis=0), "zh")
     summed = far[:, :WIDTH].sum(axis=0)

time: 128 us -> 124 us (0.969)
  blocking collectives: 85 us -> 109 us
  waiting for transfers between devices: 15.2 us -> 0.01 us
  starting transfers between devices: 17.1 us -> 5.65 us
  Pallas kernels: 6.16 us -> 7.82 us
  local copies, waits for them, and re-layouts: 1.96 us -> 0.37 us
    all_to_all x5 -> x6, blocking collectives: 85 us -> 109 us  [swapped(): return lax.all_to_all(array, axes, 0, 0, tiled=True)]
    all_to_all x1 -> x0, waiting for transfers between devices: 14.1 us -> none  [swapped(): return lax.all_to_all(array, axes, 0, 0, tiled=True)]
    all_to_all x1 -> x0, starting transfers between devices: 11.4 us -> none  [swapped(): return lax.all_to_all(array, axes, 0, 0, tiled=True)]
    pallas_call x0 -> x2, Pallas kernels: none -> 1.66 us  [the longest x1 1.6 us: staged(): pl.pallas_call(staging_kernel, in_specs=[pl.BlockSpec(memory_space=pltpu....]
    unnamed x4 -> x0, local copies, waits for them, and re-layouts: 1.6 us -> none
  transfers between devices with their start and end apart: 2 -> 1, of which waited for: 2 -> 0; matrix products, arithmetic and copies ran while one was open for 0% -> 0% of each run, Pallas kernels for 0% -> 1%
where the time goes in v3:
time: 124 us
  blocking collectives  109 us (88%)
  Pallas kernels  7.82 us (6%)
  starting transfers between devices  5.65 us (5%)
    all_to_all x6, blocking collectives, swapped(): return lax.all_to_all(array, axes, 0, 0, tiled=True)  109 us
    ppermute x1, starting transfers between devices, on_device(): columns = lax.ppermute(half, AXES, column_routes())  5.65 us
    pallas_call x1, Pallas kernels, last_step(): pl.pallas_call(last_kernel, in_specs=in_vmem(4), out_specs=pl.BlockSpec(m...  3.58 us
  transfers between devices with their start and end apart: 1, of which 0 were waited for; matrix products, arithmetic and copies ran while one was open for 0% of the time, Pallas kernels for 1%

profile of v3, /device:TPU:1, one launch (start us, length us, event | category | flops | bytes accessed | tf_op | source)
XLA Modules:
  0.0 123.9 jit_solution(9129300882160917826)
XLA Ops:
  0.0 0.9 select_select_fusion
  1.0 5.7 %collective-permute-start = (f32[64,128]{1,0:T(8,128)S(1)}, f32[64,128]{1,0:T(8,128)S(1)}, u32[]{:S(2)}, u32[]{:S(2)}) collective-permute-start(f32[64,128]{1,0:T(8,128)S(1)} %constant_dynamic-slice_fusion), channel_id=1, source_target_pairs={{0,256},{1,257},{2,128},{3,129},{4,0},{5,1},{6,384},{7,385},{8,386... | collective-permute-start | bytes 98312 | tf_op jit(solution)/shard_map/ppermute | solution.py:257
  6.6 1.6 %staging.1.matrix_ref = f32[4096,128]{1,0:T(8,128)S(1)} custom-call(f32[4096,128]{1,0:T(8,128)} %matrix_ref.1), custom_call_target="tpu_custom_call" | custom-call | tf_op jit(solution)/shard_map/staging/pallas_call | solution.py:89
  8.2 0.0 collective-permute-done.columns_ref
  8.3 0.9 value.1
  9.1 11.1 %all_to_all.30.pair_ref = f32[2,16,64,128]{3,2,1,0:T(8,128)S(1)} all-to-all(f32[2,16,64,128]{3,2,1,0:T(8,128)S(1)} %bitcast.11), channel_id=1, replica_groups=mesh['row'=4,'zh'=4,'zl'=4,'x'=4,'core'=2] {'core'}, dimensions={0} | all-to-all | bytes 2097152 | tf_op jit(solution)/shard_map/all_to_all | solution.py:38
  20.2 0.1 pair.1
  20.3 25.3 %all_to_all.31 = f32[16,64,128]{2,1,0:T(8,128)S(1)} all-to-all(f32[16,64,128]{2,1,0:T(8,128)S(1)} %pair.1), channel_id=1, replica_groups=mesh['row'=4,'zh'=4,'zl'=4,'x'=4,'core'=2] {'zl','x'}, dimensions={0} | all-to-all | bytes 1048576 | tf_op jit(solution)/shard_map/all_to_all | solution.py:38
  45.7 24.7 %all_to_all.32 = f32[4,80,128]{2,1,0:T(8,128)S(1)} all-to-all(f32[4,80,128]{2,1,0:T(8,128)S(1)} %broadcast_in_dim.21), channel_id=1, replica_groups=mesh['row'=4,'zh'=4,'zl'=4,'x'=4,'core'=2] {'zh'}, dimensions={0} | all-to-all | bytes 327680 | tf_op jit(solution)/shard_map/all_to_all | solution.py:38
  70.4 0.1 broadcast_in_dim.22
  70.5 29.5 %all_to_all.33 = f32[16,128,128]{2,1,0:T(8,128)S(1)} all-to-all(f32[16,128,128]{2,1,0:T(8,128)S(1)} %broadcast_in_dim.22), channel_id=1, replica_groups=mesh['row'=4,'zh'=4,'zl'=4,'x'=4,'core'=2] {'zl','x'}, dimensions={0} | all-to-all | bytes 2097152 | tf_op jit(solution)/shard_map/all_to_all | solution.py:38
  100.0 0.2 broadcast_in_dim.23
  100.3 8.6 %all_to_all.34 = f32[2,16,128,128]{3,2,1,0:T(8,128)S(1)} all-to-all(f32[2,16,128,128]{3,2,1,0:T(8,128)S(1)} %broadcast_in_dim.23), channel_id=1, replica_groups=mesh['row'=4,'zh'=4,'zl'=4,'x'=4,'core'=2] {'core'}, dimensions={0} | all-to-all | bytes 4194304 | tf_op jit(solution)/shard_map/all_to_all | solution.py:38
  108.9 1.7 %terms.1 = f32[4,64,256]{2,1,0:T(8,128)S(1)} custom-call(f32[2,4,4,128,128]{4,3,2,1,0:T(8,128)S(1)} %bitcast.9, f32[4096,128]{1,0:T(8,128)S(1)} %staging.1.matrix_ref), custom_call_target="tpu_custom_call" | custom-call | tf_op jit(solution)/shard_map/terms/pallas_call | solution.py:184
  110.6 9.8 %all_to_all.35.parts_ref = f32[4,64,256]{2,1,0:T(8,128)S(1)} all-to-all(f32[4,64,256]{2,1,0:T(8,128)S(1)} %terms.1), channel_id=1, replica_groups=mesh['row'=4,'zh'=4,'zl'=4,'x'=4,'core'=2] {'row'}, dimensions={0} | all-to-all | bytes 524288 | tf_op jit(solution)/shard_map/all_to_all | solution.py:38
  120.3 3.6 %last.1 = f32[4096,128]{1,0:T(8,128)} custom-call(f32[4,64,256]{2,1,0:T(8,128)S(1)} %all_to_all.35.parts_ref, f32[64,128]{1,0:T(8,128)S(1)} %collective-permute-done.columns_ref, f32[2,4,4,128,128]{4,3,2,1,0:T(8,128)S(1)} %bitcast.10, f32[4096,128]{1,0:T(8,128)S(1)} %staging.1.matrix_ref), custom_call_target="tpu_custom_call" | custom-call | tf_op jit(solution)/shard_map/last/pallas_call | solution.py:238
  (10 shorter events, 0.1 us)
Async XLA Ops:
  1.0 7.3 %collective-permute-start = (f32[64,128]{1,0:T(8,128)S(1)}, f32[64,128]{1,0:T(8,128)S(1)}, u32[]{:S(2)}, u32[]{:S(2)}) collective-permute-start(f32[64,128]{1,0:T(8,128)S(1)} %constant_dynamic-slice_fusion), channel_id=1, source_target_pairs={{0,256},{1,257},{2,128},{3,129},{4,0},{5,1},{6,384},{7,385},{8,386... | collective-permute-start | bytes 98312 | tf_op jit(solution)/shard_map/ppermute | solution.py:257

commit v4 on v3

--- a/solution.py
+++ b/solution.py
@@ -138,13 +138,13 @@
 def reflector_block(joined_ref, unit, half):
     zh, zl = divmod(unit, 4)
     start = WIDTH + zh * 16 + half * 8
-    return joined_ref[:, zl, :, start : start + 8, :].reshape(WIDTH, LANES)
+    return joined_ref[:, :, zl, start : start + 8, :].reshape(WIDTH, LANES)
 
 
 def value_unit(joined_ref, unit):
     piece = 2 * unit
     core, zl, x = piece // 16, piece // 4 % 4, piece % 4
-    return joined_ref[core, zl, x : x + 2, :WIDTH, :].reshape(2 * WIDTH, LANES)
+    return joined_ref[core, x : x + 2, zl, :WIDTH, :].reshape(2 * WIDTH, LANES)
 
 
 def in_three(array):
@@ -266,8 +266,7 @@
     far = shared(jnp.concatenate([values, lines], axis=0), "zh")
     summed = far[:, :WIDTH].sum(axis=0)
     own = jnp.concatenate([summed, far[:, WIDTH:].reshape(WIDTH, LANES)], axis=0)
-    joined = shared(shared(own, PLANE), "core")
-    joined = local(joined.reshape(2, 4, 4, 2 * WIDTH, LANES))
+    joined = local(shared(shared(shared(own, "zl"), "x"), "core"))
 
     parts = local(swapped(left_parts(joined, matrix), "row"))
     return last_step(parts, columns, joined, matrix)

time: 124 us -> 120 us (0.968)
  blocking collectives: 109 us -> 105 us
    all_to_all x6 -> x7, blocking collectives: 109 us -> 105 us  [swapped(): return lax.all_to_all(array, axes, 0, 0, tiled=True)]
where the time goes in v4:
time: 120 us
  blocking collectives  105 us (88%)
  Pallas kernels  7.82 us (7%)
  starting transfers between devices  5.65 us (5%)
    all_to_all x7, blocking collectives, swapped(): return lax.all_to_all(array, axes, 0, 0, tiled=True)  105 us
    ppermute x1, starting transfers between devices, on_device(): columns = lax.ppermute(half, AXES, column_routes())  5.65 us
    pallas_call x1, Pallas kernels, last_step(): pl.pallas_call(last_kernel, in_specs=in_vmem(4), out_specs=pl.BlockSpec(m...  3.59 us
  transfers between devices with their start and end apart: 1, of which 0 were waited for; matrix products, arithmetic and copies ran while one was open for 0% of the time, Pallas kernels for 1%

profile of v4, /device:TPU:1, one launch (start us, length us, event | category | flops | bytes accessed | tf_op | source)
XLA Modules:
  0.0 119.8 jit_solution(12281447014116059609)
XLA Ops:
  0.0 0.9 select_select_fusion
  1.0 5.7 %collective-permute-start = (f32[64,128]{1,0:T(8,128)S(1)}, f32[64,128]{1,0:T(8,128)S(1)}, u32[]{:S(2)}, u32[]{:S(2)}) collective-permute-start(f32[64,128]{1,0:T(8,128)S(1)} %constant_dynamic-slice_fusion), channel_id=1, source_target_pairs={{0,256},{1,257},{2,128},{3,129},{4,0},{5,1},{6,384},{7,385},{8,386... | collective-permute-start | bytes 98312 | tf_op jit(solution)/shard_map/ppermute | solution.py:257
  6.6 1.6 %staging.1.matrix_ref = f32[4096,128]{1,0:T(8,128)S(1)} custom-call(f32[4096,128]{1,0:T(8,128)} %matrix_ref.1), custom_call_target="tpu_custom_call" | custom-call | tf_op jit(solution)/shard_map/staging/pallas_call | solution.py:89
  8.2 0.0 collective-permute-done.columns_ref
  8.3 0.9 value.1
  9.1 11.1 %all_to_all.35.pair_ref = f32[2,16,64,128]{3,2,1,0:T(8,128)S(1)} all-to-all(f32[2,16,64,128]{3,2,1,0:T(8,128)S(1)} %bitcast.8), channel_id=1, replica_groups=mesh['row'=4,'zh'=4,'zl'=4,'x'=4,'core'=2] {'core'}, dimensions={0} | all-to-all | bytes 2097152 | tf_op jit(solution)/shard_map/all_to_all | solution.py:38
  20.2 0.1 pair.1
  20.3 25.3 %all_to_all.36 = f32[16,64,128]{2,1,0:T(8,128)S(1)} all-to-all(f32[16,64,128]{2,1,0:T(8,128)S(1)} %pair.1), channel_id=1, replica_groups=mesh['row'=4,'zh'=4,'zl'=4,'x'=4,'core'=2] {'zl','x'}, dimensions={0} | all-to-all | bytes 1048576 | tf_op jit(solution)/shard_map/all_to_all | solution.py:38
  45.7 24.7 %all_to_all.37 = f32[4,80,128]{2,1,0:T(8,128)S(1)} all-to-all(f32[4,80,128]{2,1,0:T(8,128)S(1)} %broadcast_in_dim.24), channel_id=1, replica_groups=mesh['row'=4,'zh'=4,'zl'=4,'x'=4,'core'=2] {'zh'}, dimensions={0} | all-to-all | bytes 327680 | tf_op jit(solution)/shard_map/all_to_all | solution.py:38
  70.4 10.4 %all_to_all.38 = f32[4,128,128]{2,1,0:T(8,128)S(1)} all-to-all(f32[4,128,128]{2,1,0:T(8,128)S(1)} %broadcast_in_dim.25), channel_id=1, replica_groups=mesh['row'=4,'zh'=4,'zl'=4,'x'=4,'core'=2] {'zl'}, dimensions={0} | all-to-all | bytes 524288 | tf_op jit(solution)/shard_map/all_to_all | solution.py:38
  80.9 0.1 broadcast_in_dim.26
  81.0 13.0 %all_to_all.39 = f32[4,4,128,128]{3,2,1,0:T(8,128)S(1)} all-to-all(f32[4,4,128,128]{3,2,1,0:T(8,128)S(1)} %broadcast_in_dim.26), channel_id=1, replica_groups=mesh['row'=4,'zh'=4,'zl'=4,'x'=4,'core'=2] {'x'}, dimensions={0} | all-to-all | bytes 2097152 | tf_op jit(solution)/shard_map/all_to_all | solution.py:38
  94.0 0.2 broadcast_in_dim.27
  94.3 10.5 %all_to_all.40.joined_ref = f32[2,4,4,128,128]{4,3,2,1,0:T(8,128)S(1)} all-to-all(f32[2,4,4,128,128]{4,3,2,1,0:T(8,128)S(1)} %broadcast_in_dim.27), channel_id=1, replica_groups=mesh['row'=4,'zh'=4,'zl'=4,'x'=4,'core'=2] {'core'}, dimensions={0} | all-to-all | bytes 4194304 | tf_op jit(solution)/shard_map/all_to_all | solution.py:38
  104.7 1.7 %terms.1 = f32[4,64,256]{2,1,0:T(8,128)S(1)} custom-call(f32[2,4,4,128,128]{4,3,2,1,0:T(8,128)S(1)} %all_to_all.40.joined_ref, f32[4096,128]{1,0:T(8,128)S(1)} %staging.1.matrix_ref), custom_call_target="tpu_custom_call" | custom-call | tf_op jit(solution)/shard_map/terms/pallas_call | solution.py:184
  106.4 9.8 %all_to_all.41.parts_ref = f32[4,64,256]{2,1,0:T(8,128)S(1)} all-to-all(f32[4,64,256]{2,1,0:T(8,128)S(1)} %terms.1), channel_id=1, replica_groups=mesh['row'=4,'zh'=4,'zl'=4,'x'=4,'core'=2] {'row'}, dimensions={0} | all-to-all | bytes 524288 | tf_op jit(solution)/shard_map/all_to_all | solution.py:38
  116.2 3.6 %last.1 = f32[4096,128]{1,0:T(8,128)} custom-call(f32[4,64,256]{2,1,0:T(8,128)S(1)} %all_to_all.41.parts_ref, f32[64,128]{1,0:T(8,128)S(1)} %collective-permute-done.columns_ref, f32[2,4,4,128,128]{4,3,2,1,0:T(8,128)S(1)} %all_to_all.40.joined_ref, f32[4096,128]{1,0:T(8,128)S(1)} %staging.1.matrix_ref), custom_call_target="tpu_custom_call" | custom-call | tf_op jit(solution)/shard_map/last/pallas_call | solution.py:238
  (11 shorter events, 0.1 us)
Async XLA Ops:
  1.0 7.3 %collective-permute-start = (f32[64,128]{1,0:T(8,128)S(1)}, f32[64,128]{1,0:T(8,128)S(1)}, u32[]{:S(2)}, u32[]{:S(2)}) collective-permute-start(f32[64,128]{1,0:T(8,128)S(1)} %constant_dynamic-slice_fusion), channel_id=1, source_target_pairs={{0,256},{1,257},{2,128},{3,129},{4,0},{5,1},{6,384},{7,385},{8,386... | collective-permute-start | bytes 98312 | tf_op jit(solution)/shard_map/ppermute | solution.py:257

commit v5 on v2

--- a/solution.py
+++ b/solution.py
@@ -79,39 +79,43 @@
     return [pl.BlockSpec(memory_space=pltpu.VMEM)] * count
 
 
-def value_kernel(columns_ref, matrix_ref, out_ref):
-    high, low = split(doubled(columns_ref[...].T))
-    right = jnp.concatenate([high, low], axis=1)
-    for unit in range(16):
-        first = matrix_ref[2 * unit * LANES : (2 * unit + 1) * LANES, :]
-        second = matrix_ref[(2 * unit + 1) * LANES : (2 * unit + 2) * LANES, :]
-        high, low = split(jnp.concatenate([first, second], axis=1))
-        both = dot(high, right, NN) + dot(low, right, NN)
+def value_kernel(piece_ref, halves_ref, out_ref):
+    right = []
+    for half in range(2):
+        columns = piece_ref[:, half * LANES : (half + 1) * LANES].T
+        right.append(jnp.concatenate(split(doubled(columns)), axis=1))
+    for unit in range(8):
+        both = jnp.zeros((LANES, 2 * LANES), jnp.float32)
+        for half in range(2):
+            first = halves_ref[half, 2 * unit * LANES : (2 * unit + 1) * LANES, :]
+            second = halves_ref[half, (2 * unit + 1) * LANES : (2 * unit + 2) * LANES, :]
+            high, low = split(jnp.concatenate([first, second], axis=1))
+            both += dot(high, right[half], NN) + dot(low, right[half], NN)
         total = both[:, :LANES] + both[:, LANES:]
         out_ref[2 * unit : 2 * unit + 2] = total.reshape(2, WIDTH, LANES)
 
 
-def partial_value(columns, matrix):
+def half_value(piece, halves):
     return pl.pallas_call(
         value_kernel,
         in_specs=in_vmem(2),
         out_specs=in_vmem(1)[0],
-        out_shape=pltpu.VMEM((32, WIDTH, LANES), jnp.float32),
+        out_shape=pltpu.VMEM((16, WIDTH, LANES), jnp.float32),
         compiler_params=ROOM,
         name="value",
-    )(columns, matrix)
+    )(local(piece), local(halves))
 
 
 def reflector_block(joined_ref, unit, half):
     zh, zl = divmod(unit, 4)
     start = WIDTH + zh * 16 + half * 8
-    return joined_ref[:, zl, :, start : start + 8, :].reshape(WIDTH, LANES)
+    return joined_ref[:, :, zl, start : start + 8, :].reshape(WIDTH, LANES)
 
 
 def value_unit(joined_ref, unit):
     piece = 2 * unit
     core, zl, x = piece // 16, piece // 4 % 4, piece % 4
-    return joined_ref[core, zl, x : x + 2, :WIDTH, :].reshape(2 * WIDTH, LANES)
+    return joined_ref[core, x : x + 2, zl, :WIDTH, :].reshape(2 * WIDTH, LANES)
 
 
 def in_three(array):
@@ -217,23 +221,24 @@
 
 
 def on_device(matrix, vectors):
-    width, piece = vectors.shape
+    width, span = vectors.shape
     core, x = lax.axis_index("core"), lax.axis_index("x")
-    masked = mask_vectors(vectors, lax.axis_index(("row", "zh", "zl")) * piece)
-    half = lax.dynamic_slice_in_dim(masked, core * LANES, LANES, 1)
-    columns = lax.ppermute(half, AXES, column_routes())
+    halves = swapped(matrix.reshape(2, -1, LANES), "core")
+    piece = lax.ppermute(vectors, AXES, column_routes())
+    matrix = local(matrix)
+    masked = mask_vectors(vectors, lax.axis_index(("row", "zh", "zl")) * span)
     lines = lax.dynamic_slice_in_dim(masked, (core * 4 + x) * 8, 8, 0)
     lines = lines.reshape(8, 2, LANES).swapaxes(0, 1).reshape(16, LANES)
 
-    matrix, columns = local(matrix), local(columns)
-    values = partial_value(columns, matrix)
-    values = swapped(values.reshape(2, 16, WIDTH, LANES), "core").sum(axis=0)
+    piece = mask_vectors(piece, lax.axis_index(("zh", "zl", "x")) * span)
+    columns = local(lax.dynamic_slice_in_dim(piece, core * LANES, LANES, 1))
+    values = half_value(piece, halves)
+    values, lines, columns = lax.optimization_barrier((values, lines, columns))
     values = swapped(values, PLANE).sum(axis=0)
     far = shared(jnp.concatenate([values, lines], axis=0), "zh")
     summed = far[:, :WIDTH].sum(axis=0)
     own = jnp.concatenate([summed, far[:, WIDTH:].reshape(WIDTH, LANES)], axis=0)
-    joined = shared(shared(own, PLANE), "core")
-    joined = local(joined.reshape(2, 4, 4, 2 * WIDTH, LANES))
+    joined = local(shared(shared(shared(own, "zl"), "x"), "core"))
 
     parts = local(swapped(left_parts(joined, matrix), "row"))
     return last_step(parts, columns, joined, matrix)

time: 128 us -> 124 us (0.969)
  blocking collectives: 85 us -> 98.6 us
  waiting for transfers between devices: 15.2 us -> 4.96 us
  starting transfers between devices: 17.1 us -> 12.7 us
  other arithmetic: 1.88 us -> 0.22 us
  local copies, waits for them, and re-layouts: 1.96 us -> 0.47 us
    all_to_all x1, waiting for transfers between devices: 14.1 us -> 0.01 us  [swapped(): return lax.all_to_all(array, axes, 0, 0, tiled=True)]
    all_to_all x5 -> x6, blocking collectives: 85 us -> 98.6 us  [swapped(): return lax.all_to_all(array, axes, 0, 0, tiled=True)]
    ppermute x1, waiting for transfers between devices: 1.12 us -> 4.95 us  [on_device(): piece = lax.ppermute(vectors, AXES, column_routes())]
    ppermute x1, starting transfers between devices: 5.65 us -> 1.91 us  [on_device(): piece = lax.ppermute(vectors, AXES, column_routes())]
    unnamed x4, local copies, waits for them, and re-layouts: 1.6 us -> 0.01 us
  transfers between devices with their start and end apart: 2 -> 2, of which waited for: 2 -> 1; matrix products, arithmetic and copies ran while one was open for 0% -> 0% of each run, Pallas kernels for 0% -> 0%
where the time goes in v5:
time: 124 us; the launch traced here: 123 us
  blocking collectives  98.6 us (80%)
  starting transfers between devices  12.7 us (10%)
  Pallas kernels  6.23 us (5%)
  waiting for transfers between devices  4.96 us (4%)
    all_to_all x6, blocking collectives, swapped(): return lax.all_to_all(array, axes, 0, 0, tiled=True)  98.6 us
    all_to_all x1, starting transfers between devices, swapped(): return lax.all_to_all(array, axes, 0, 0, tiled=True)  10.8 us
    ppermute x1, waiting for transfers between devices, on_device(): piece = lax.ppermute(vectors, AXES, column_routes())  4.95 us
    pallas_call x1, Pallas kernels, last_step(): pl.pallas_call(last_kernel, in_specs=in_vmem(4), out_specs=pl.BlockSpec(m...  3.58 us
  transfers between devices with their start and end apart: 2, of which 1 were waited for; matrix products, arithmetic and copies ran while one was open for 0% of the time, Pallas kernels for 0%

profile of v5, /device:TPU:1, one launch (start us, length us, event | category | flops | bytes accessed | tf_op | source)
XLA Modules:
  0.0 123.3 jit_solution(9085473231619319634)
XLA Ops:
  0.0 0.0 copy-start.1
  0.0 10.8 %all-to-all-start = ((f32[2,2048,128]{2,1,0:T(8,128)}), f32[2,2048,128]{2,1,0:T(8,128)S(1)}, u32[]{:S(2)}, u32[]{:S(2)}) async-start(f32[2,2048,128]{2,1,0:T(8,128)} %bitcast.8), calls=%async_computation | async-start | bytes 4194304 | tf_op jit(solution)/shard_map/all_to_all | solution.py:38
  10.8 0.0 copy-done.1
  10.8 1.9 %collective-permute-start = (f32[64,256]{1,0:T(8,128)S(1)}, f32[64,256]{1,0:T(8,128)S(1)}, u32[]{:S(2)}, u32[]{:S(2)}) collective-permute-start(f32[64,256]{1,0:T(8,128)S(1)} %copy-done.1), channel_id=1, source_target_pairs={{0,256},{1,257},{2,128},{3,129},{4,0},{5,1},{6,384},{7,385},{8,386... | collective-permute-start | bytes 196616 | tf_op jit(solution)/shard_map/ppermute | solution.py:227
  12.7 0.1 dynamic-slice
  12.8 0.1 fusion
  12.9 5.0 %collective-permute-done = f32[64,256]{1,0:T(8,128)S(1)} collective-permute-done((f32[64,256]{1,0:T(8,128)S(1)}, f32[64,256]{1,0:T(8,128)S(1)}, u32[]{:S(2)}, u32[]{:S(2)}) %collective-permute-start) | collective-permute-done | bytes 65568 | tf_op jit(solution)/shard_map/ppermute | solution.py:227
  17.8 0.1 select_select_fusion.piece_ref
  17.9 0.0 all-to-all-done.halves_ref
  18.0 0.9 value.1
  18.9 24.7 %all_to_all.35 = f32[16,64,128]{2,1,0:T(8,128)S(1)} all-to-all(f32[16,64,128]{2,1,0:T(8,128)S(1)} %value.1), channel_id=1, replica_groups=mesh['row'=4,'zh'=4,'zl'=4,'x'=4,'core'=2] {'zl','x'}, dimensions={0} | all-to-all | bytes 1048576 | tf_op jit(solution)/shard_map/all_to_all | solution.py:38
  43.7 24.0 %all_to_all.36 = f32[4,80,128]{2,1,0:T(8,128)S(1)} all-to-all(f32[4,80,128]{2,1,0:T(8,128)S(1)} %broadcast_in_dim.28), channel_id=1, replica_groups=mesh['row'=4,'zh'=4,'zl'=4,'x'=4,'core'=2] {'zh'}, dimensions={0} | all-to-all | bytes 327680 | tf_op jit(solution)/shard_map/all_to_all | solution.py:38
  67.7 9.2 %all_to_all.37 = f32[4,128,128]{2,1,0:T(8,128)S(1)} all-to-all(f32[4,128,128]{2,1,0:T(8,128)S(1)} %broadcast_in_dim.29), channel_id=1, replica_groups=mesh['row'=4,'zh'=4,'zl'=4,'x'=4,'core'=2] {'zl'}, dimensions={0} | all-to-all | bytes 524288 | tf_op jit(solution)/shard_map/all_to_all | solution.py:38
  76.9 0.1 broadcast_in_dim.30
  77.0 12.2 %all_to_all.38 = f32[4,4,128,128]{3,2,1,0:T(8,128)S(1)} all-to-all(f32[4,4,128,128]{3,2,1,0:T(8,128)S(1)} %broadcast_in_dim.30), channel_id=1, replica_groups=mesh['row'=4,'zh'=4,'zl'=4,'x'=4,'core'=2] {'x'}, dimensions={0} | all-to-all | bytes 2097152 | tf_op jit(solution)/shard_map/all_to_all | solution.py:38
  89.2 0.2 broadcast_in_dim.31
  89.4 0.0 copy-start
  89.5 12.8 %all_to_all.39.joined_ref = f32[2,4,4,128,128]{4,3,2,1,0:T(8,128)S(1)} all-to-all(f32[2,4,4,128,128]{4,3,2,1,0:T(8,128)S(1)} %broadcast_in_dim.31), channel_id=1, replica_groups=mesh['row'=4,'zh'=4,'zl'=4,'x'=4,'core'=2] {'core'}, dimensions={0} | all-to-all | bytes 4194304 | tf_op jit(solution)/shard_map/all_to_all | solution.py:38
  102.3 0.0 copy-done
  102.3 1.7 %terms.1 = f32[4,64,256]{2,1,0:T(8,128)S(1)} custom-call(f32[2,4,4,128,128]{4,3,2,1,0:T(8,128)S(1)} %all_to_all.39.joined_ref, f32[4096,128]{1,0:T(8,128)S(1)} %copy-done), custom_call_target="tpu_custom_call" | custom-call | tf_op jit(solution)/shard_map/terms/pallas_call | solution.py:155
  104.0 15.7 %all_to_all.40.parts_ref = f32[4,64,256]{2,1,0:T(8,128)S(1)} all-to-all(f32[4,64,256]{2,1,0:T(8,128)S(1)} %terms.1), channel_id=1, replica_groups=mesh['row'=4,'zh'=4,'zl'=4,'x'=4,'core'=2] {'row'}, dimensions={0} | all-to-all | bytes 524288 | tf_op jit(solution)/shard_map/all_to_all | solution.py:38
  119.7 3.6 %last.1 = f32[4096,128]{1,0:T(8,128)} custom-call(f32[4,64,256]{2,1,0:T(8,128)S(1)} %all_to_all.40.parts_ref, f32[64,128]{1,0:T(8,128)S(1)} %constant_dynamic-slice_fusion.columns_ref, f32[2,4,4,128,128]{4,3,2,1,0:T(8,128)S(1)} %all_to_all.39.joined_ref, f32[4096,128]{1,0:T(8,128)S(1)} %copy-done), custom_call_target="tpu_custom_call" | custom-call | tf_op jit(solution)/shard_map/last/pallas_call | solution.py:209
  (11 shorter events, 0.1 us)
Async XLA Ops:
  0.0 10.8 %copy-start.1 = (f32[64,256]{1,0:T(8,128)S(1)}, f32[64,256]{1,0:T(8,128)}, u32[]{:S(2)}) copy-start(f32[64,256]{1,0:T(8,128)} %param.3) | copy-start | bytes 196612
  0.0 17.9 %all-to-all-start = ((f32[2,2048,128]{2,1,0:T(8,128)}), f32[2,2048,128]{2,1,0:T(8,128)S(1)}, u32[]{:S(2)}, u32[]{:S(2)}) async-start(f32[2,2048,128]{2,1,0:T(8,128)} %bitcast.8), calls=%async_computation | async-start | bytes 4194304 | tf_op jit(solution)/shard_map/all_to_all | solution.py:38
  10.8 7.1 %collective-permute-start = (f32[64,256]{1,0:T(8,128)S(1)}, f32[64,256]{1,0:T(8,128)S(1)}, u32[]{:S(2)}, u32[]{:S(2)}) collective-permute-start(f32[64,256]{1,0:T(8,128)S(1)} %copy-done.1), channel_id=1, source_target_pairs={{0,256},{1,257},{2,128},{3,129},{4,0},{5,1},{6,384},{7,385},{8,386... | collective-permute-start | bytes 196616 | tf_op jit(solution)/shard_map/ppermute | solution.py:227
  89.4 12.8 %copy-start = (f32[4096,128]{1,0:T(8,128)S(1)}, f32[4096,128]{1,0:T(8,128)}, u32[]{:S(2)}) copy-start(f32[4096,128]{1,0:T(8,128)} %matrix_ref.3) | copy-start | bytes 6291460

commit v6 on v4

--- a/solution.py
+++ b/solution.py
@@ -8,7 +8,6 @@
 
 AXES = ("row", "zh", "zl", "x", "core")
 COLUMNS = ("zh", "zl", "x", "core")
-PLANE = ("zl", "x")
 LANES = 128
 WIDTH = 64
 ROOM = pltpu.CompilerParams(vmem_limit_bytes=16 * 1024 * 1024)
@@ -97,6 +96,42 @@
     )(pltpu.with_memory_space_constraint(matrix, pltpu.HBM))
 
 
+def sum_kernel(parts_ref, out_ref):
+    parts = [parts_ref[k] for k in range(parts_ref.shape[0])]
+    while len(parts) > 1:
+        parts = [parts[k] + parts[k + 1] for k in range(0, len(parts), 2)]
+    out_ref[...] = parts[0]
+
+
+def summed(parts):
+    return pl.pallas_call(
+        sum_kernel,
+        in_specs=in_vmem(1),
+        out_specs=in_vmem(1)[0],
+        out_shape=pltpu.VMEM(parts.shape[1:], jnp.float32),
+        compiler_params=ROOM,
+        name="sum",
+    )(local(parts))
+
+
+def staging_kernel(matrix_ref, out_ref, sem):
+    copy = pltpu.make_async_copy(matrix_ref, out_ref, sem)
+    copy.start()
+    copy.wait()
+
+
+def staged(matrix):
+    return pl.pallas_call(
+        staging_kernel,
+        in_specs=[pl.BlockSpec(memory_space=pltpu.HBM)],
+        out_specs=in_vmem(1)[0],
+        out_shape=pltpu.VMEM(matrix.shape, jnp.float32),
+        scratch_shapes=[pltpu.SemaphoreType.DMA],
+        compiler_params=ROOM,
+        name="staging",
+    )(pltpu.with_memory_space_constraint(matrix, pltpu.HBM))
+
+
 def pair_kernel(pair_ref, out_ref):
     out_ref[...] = pair_ref[0] + pair_ref[1]
 
@@ -121,7 +156,9 @@
         high, low = split(jnp.concatenate([first, second], axis=1))
         both = dot(high, right, NN) + dot(low, right, NN)
         total = both[:, :LANES] + both[:, LANES:]
-        out_ref[2 * unit : 2 * unit + 2] = total.reshape(2, WIDTH, LANES)
+        for half in range(2):
+            core, zl, x = (2 * unit + half) // 16, unit // 2 % 4, (2 * unit + half) % 4
+            out_ref[core, x, zl] = total[half * WIDTH : (half + 1) * WIDTH]
 
 
 def partial_value(columns, matrix):
@@ -129,7 +166,7 @@
         value_kernel,
         in_specs=in_vmem(2),
         out_specs=in_vmem(1)[0],
-        out_shape=pltpu.VMEM((32, WIDTH, LANES), jnp.float32),
+        out_shape=pltpu.VMEM((2, 4, 4, WIDTH, LANES), jnp.float32),
         compiler_params=ROOM,
         name="value",
     )(columns, matrix)
@@ -260,12 +297,12 @@
 
     matrix, columns = staged(matrix), local(columns)
     values = partial_value(columns, matrix)
-    values = pair_summed(swapped(values.reshape(2, 16, WIDTH, LANES), "core"))
+    values = summed(swapped(values, "core"))
     values, lines = lax.optimization_barrier((values, lines))
-    values = swapped(values, PLANE).sum(axis=0)
+    values = summed(swapped(summed(swapped(values, "x")), "zl"))
     far = shared(jnp.concatenate([values, lines], axis=0), "zh")
-    summed = far[:, :WIDTH].sum(axis=0)
-    own = jnp.concatenate([summed, far[:, WIDTH:].reshape(WIDTH, LANES)], axis=0)
+    near = far[:, :WIDTH].sum(axis=0)
+    own = jnp.concatenate([near, far[:, WIDTH:].reshape(WIDTH, LANES)], axis=0)
     joined = local(shared(shared(shared(own, "zl"), "x"), "core"))
 
     parts = local(swapped(left_parts(joined, matrix), "row"))

time: 120 us -> 121 us (level)
    all_to_all x7 -> x8, blocking collectives: 105 us -> 105 us  [swapped(): return lax.all_to_all(array, axes, 0, 0, tiled=True)]
where the time goes in v6:
time: 121 us; the launch traced here: 120 us
  blocking collectives  105 us (87%)
  Pallas kernels  7.86 us (6%)
  starting transfers between devices  5.65 us (5%)
    all_to_all x8, blocking collectives, swapped(): return lax.all_to_all(array, axes, 0, 0, tiled=True)  105 us
    ppermute x1, starting transfers between devices, on_device(): columns = lax.ppermute(half, AXES, column_routes())  5.65 us
    pallas_call x1, Pallas kernels, last_step(): pl.pallas_call(last_kernel, in_specs=in_vmem(4), out_specs=pl.BlockSpec(m...  3.58 us
  transfers between devices with their start and end apart: 1, of which 0 were waited for; matrix products, arithmetic and copies ran while one was open for 0% of the time, Pallas kernels for 1%

profile of v6, /device:TPU:1, one launch (start us, length us, event | category | flops | bytes accessed | tf_op | source)
XLA Modules:
  0.0 120.2 jit_solution(4335313016299209876)
XLA Ops:
  0.0 0.9 select_select_fusion
  1.0 5.7 %collective-permute-start = (f32[64,128]{1,0:T(8,128)S(1)}, f32[64,128]{1,0:T(8,128)S(1)}, u32[]{:S(2)}, u32[]{:S(2)}) collective-permute-start(f32[64,128]{1,0:T(8,128)S(1)} %constant_dynamic-slice_fusion), channel_id=1, source_target_pairs={{0,256},{1,257},{2,128},{3,129},{4,0},{5,1},{6,384},{7,385},{8,386... | collective-permute-start | bytes 98312 | tf_op jit(solution)/shard_map/ppermute | solution.py:294
  6.6 1.6 %staging.1.matrix_ref = f32[4096,128]{1,0:T(8,128)S(1)} custom-call(f32[4096,128]{1,0:T(8,128)} %matrix_ref.1), custom_call_target="tpu_custom_call" | custom-call | tf_op jit(solution)/shard_map/staging/pallas_call | solution.py:124
  8.2 0.0 collective-permute-done.columns_ref
  8.3 0.9 value.1
  9.1 11.1 %all_to_all.40.parts_ref = f32[2,4,4,64,128]{4,3,2,1,0:T(8,128)S(1)} all-to-all(f32[2,4,4,64,128]{4,3,2,1,0:T(8,128)S(1)} %value.1), channel_id=1, replica_groups=mesh['row'=4,'zh'=4,'zl'=4,'x'=4,'core'=2] {'core'}, dimensions={0} | all-to-all | bytes 2097152 | tf_op jit(solution)/shard_map/all_to_all | solution.py:37
  20.2 0.1 sum.3
  20.3 11.6 %all_to_all.41.parts_ref = f32[4,4,64,128]{3,2,1,0:T(8,128)S(1)} all-to-all(f32[4,4,64,128]{3,2,1,0:T(8,128)S(1)} %sum.3), channel_id=1, replica_groups=mesh['row'=4,'zh'=4,'zl'=4,'x'=4,'core'=2] {'x'}, dimensions={0} | all-to-all | bytes 1048576 | tf_op jit(solution)/shard_map/all_to_all | solution.py:37
  31.9 14.2 %all_to_all.42.parts_ref = f32[4,64,128]{2,1,0:T(8,128)S(1)} all-to-all(f32[4,64,128]{2,1,0:T(8,128)S(1)} %sum.4), channel_id=1, replica_groups=mesh['row'=4,'zh'=4,'zl'=4,'x'=4,'core'=2] {'zl'}, dimensions={0} | all-to-all | bytes 262144 | tf_op jit(solution)/shard_map/all_to_all | solution.py:37
  46.2 25.6 %all_to_all.43 = f32[4,80,128]{2,1,0:T(8,128)S(1)} all-to-all(f32[4,80,128]{2,1,0:T(8,128)S(1)} %broadcast_in_dim.24), channel_id=1, replica_groups=mesh['row'=4,'zh'=4,'zl'=4,'x'=4,'core'=2] {'zh'}, dimensions={0} | all-to-all | bytes 327680 | tf_op jit(solution)/shard_map/all_to_all | solution.py:37
  71.8 8.4 %all_to_all.44 = f32[4,128,128]{2,1,0:T(8,128)S(1)} all-to-all(f32[4,128,128]{2,1,0:T(8,128)S(1)} %broadcast_in_dim.25), channel_id=1, replica_groups=mesh['row'=4,'zh'=4,'zl'=4,'x'=4,'core'=2] {'zl'}, dimensions={0} | all-to-all | bytes 524288 | tf_op jit(solution)/shard_map/all_to_all | solution.py:37
  80.2 0.1 broadcast_in_dim.26
  80.3 12.2 %all_to_all.45 = f32[4,4,128,128]{3,2,1,0:T(8,128)S(1)} all-to-all(f32[4,4,128,128]{3,2,1,0:T(8,128)S(1)} %broadcast_in_dim.26), channel_id=1, replica_groups=mesh['row'=4,'zh'=4,'zl'=4,'x'=4,'core'=2] {'x'}, dimensions={0} | all-to-all | bytes 2097152 | tf_op jit(solution)/shard_map/all_to_all | solution.py:37
  92.4 0.2 broadcast_in_dim.27
  92.7 12.5 %all_to_all.46.joined_ref = f32[2,4,4,128,128]{4,3,2,1,0:T(8,128)S(1)} all-to-all(f32[2,4,4,128,128]{4,3,2,1,0:T(8,128)S(1)} %broadcast_in_dim.27), channel_id=1, replica_groups=mesh['row'=4,'zh'=4,'zl'=4,'x'=4,'core'=2] {'core'}, dimensions={0} | all-to-all | bytes 4194304 | tf_op jit(solution)/shard_map/all_to_all | solution.py:37
  105.2 1.7 %terms.1 = f32[4,64,256]{2,1,0:T(8,128)S(1)} custom-call(f32[2,4,4,128,128]{4,3,2,1,0:T(8,128)S(1)} %all_to_all.46.joined_ref, f32[4096,128]{1,0:T(8,128)S(1)} %staging.1.matrix_ref), custom_call_target="tpu_custom_call" | custom-call | tf_op jit(solution)/shard_map/terms/pallas_call | solution.py:221
  106.9 9.8 %all_to_all.47.parts_ref = f32[4,64,256]{2,1,0:T(8,128)S(1)} all-to-all(f32[4,64,256]{2,1,0:T(8,128)S(1)} %terms.1), channel_id=1, replica_groups=mesh['row'=4,'zh'=4,'zl'=4,'x'=4,'core'=2] {'row'}, dimensions={0} | all-to-all | bytes 524288 | tf_op jit(solution)/shard_map/all_to_all | solution.py:37
  116.6 3.6 %last.1 = f32[4096,128]{1,0:T(8,128)} custom-call(f32[4,64,256]{2,1,0:T(8,128)S(1)} %all_to_all.47.parts_ref, f32[64,128]{1,0:T(8,128)S(1)} %collective-permute-done.columns_ref, f32[2,4,4,128,128]{4,3,2,1,0:T(8,128)S(1)} %all_to_all.46.joined_ref, f32[4096,128]{1,0:T(8,128)S(1)} %staging.1.matrix_ref), custom_call_target="tpu_custom_call" | custom-call | tf_op jit(solution)/shard_map/last/pallas_call | solution.py:275
  (12 shorter events, 0.1 us)
Async XLA Ops:
  1.0 7.3 %collective-permute-start = (f32[64,128]{1,0:T(8,128)S(1)}, f32[64,128]{1,0:T(8,128)S(1)}, u32[]{:S(2)}, u32[]{:S(2)}) collective-permute-start(f32[64,128]{1,0:T(8,128)S(1)} %constant_dynamic-slice_fusion), channel_id=1, source_target_pairs={{0,256},{1,257},{2,128},{3,129},{4,0},{5,1},{6,384},{7,385},{8,386... | collective-permute-start | bytes 98312 | tf_op jit(solution)/shard_map/ppermute | solution.py:294

commit v7 on v4

--- a/solution.py
+++ b/solution.py
@@ -112,8 +112,11 @@
     )(local(pair))
 
 
-def value_kernel(columns_ref, matrix_ref, out_ref):
-    high, low = split(doubled(columns_ref[...].T))
+def value_kernel(place_ref, piece_ref, matrix_ref, out_ref, columns_ref):
+    start = pl.multiple_of(place_ref[0] * LANES, LANES)
+    columns = mask_vectors(piece_ref[:, pl.ds(start, LANES)], place_ref[1])
+    columns_ref[...] = columns
+    high, low = split(doubled(columns.T))
     right = jnp.concatenate([high, low], axis=1)
     for unit in range(16):
         first = matrix_ref[2 * unit * LANES : (2 * unit + 1) * LANES, :]
@@ -124,27 +127,34 @@
         out_ref[2 * unit : 2 * unit + 2] = total.reshape(2, WIDTH, LANES)
 
 
-def partial_value(columns, matrix):
+def partial_value(place, piece, matrix):
     return pl.pallas_call(
         value_kernel,
-        in_specs=in_vmem(2),
-        out_specs=in_vmem(1)[0],
-        out_shape=pltpu.VMEM((32, WIDTH, LANES), jnp.float32),
+        in_specs=[pl.BlockSpec(memory_space=pltpu.SMEM), *in_vmem(2)],
+        out_specs=in_vmem(2),
+        out_shape=[
+            pltpu.VMEM((32, WIDTH, LANES), jnp.float32),
+            pltpu.VMEM((WIDTH, LANES), jnp.float32),
+        ],
         compiler_params=ROOM,
         name="value",
-    )(columns, matrix)
-
-
-def reflector_block(joined_ref, unit, half):
+    )(place, local(piece), matrix)
+
+
+def reflector_block(core, own_ref, other_ref, unit, half):
     zh, zl = divmod(unit, 4)
     start = WIDTH + zh * 16 + half * 8
-    return joined_ref[:, :, zl, start : start + 8, :].reshape(WIDTH, LANES)
-
-
-def value_unit(joined_ref, unit):
+    own = own_ref[:, zl, start : start + 8, :].reshape(WIDTH // 2, LANES)
+    other = other_ref[:, zl, start : start + 8, :].reshape(WIDTH // 2, LANES)
+    first = jnp.where(core == 0, own, other)
+    return jnp.concatenate([first, jnp.where(core == 0, other, own)], axis=0)
+
+
+def value_unit(core, own_ref, other_ref, unit):
     piece = 2 * unit
-    core, zl, x = piece // 16, piece // 4 % 4, piece % 4
-    return joined_ref[core, x : x + 2, zl, :WIDTH, :].reshape(2 * WIDTH, LANES)
+    zl, x = piece // 4 % 4, piece % 4
+    own, other = own_ref[x : x + 2, zl, :WIDTH, :], other_ref[x : x + 2, zl, :WIDTH, :]
+    return jnp.where(core == piece // 16, own, other).reshape(2 * WIDTH, LANES)
 
 
 def in_three(array):
@@ -153,17 +163,18 @@
     return jnp.concatenate([high, low, rest.astype(jnp.bfloat16)], axis=0)
 
 
-def terms_kernel(joined_ref, matrix_ref, out_ref):
+def terms_kernel(place_ref, own_ref, other_ref, matrix_ref, out_ref):
+    held = (place_ref[0], own_ref, other_ref)
     plain = jnp.zeros((2 * WIDTH, 2 * LANES), jnp.float32)
     cross = jnp.zeros((4 * WIDTH, 2 * LANES), jnp.float32)
     gram = jnp.zeros((3 * WIDTH, 3 * WIDTH), jnp.float32)
     for unit in range(16):
-        rows = [reflector_block(joined_ref, unit, half) for half in range(2)]
+        rows = [reflector_block(*held, unit, half) for half in range(2)]
         rows = in_three(jnp.concatenate(rows, axis=1))
         span = slice(2 * unit * LANES, 2 * (unit + 1) * LANES)
         right = jnp.concatenate(split(matrix_ref[span, :]), axis=1)
         plain += dot(rows[: 2 * WIDTH], right, NN)
-        right = jnp.concatenate(split(value_unit(joined_ref, unit)), axis=1)
+        right = jnp.concatenate(split(value_unit(*held, unit)), axis=1)
         both = [rows[: 2 * WIDTH, :LANES], rows[: 2 * WIDTH, LANES:]]
         cross += dot(jnp.concatenate(both, axis=0), right, NN)
         gram += dot(rows, rows, NT)
@@ -180,15 +191,15 @@
         out_ref[y] = joined
 
 
-def left_parts(joined, matrix):
+def left_parts(place, own, other, matrix):
     return pl.pallas_call(
         terms_kernel,
-        in_specs=in_vmem(2),
+        in_specs=[pl.BlockSpec(memory_space=pltpu.SMEM), *in_vmem(3)],
         out_specs=in_vmem(1)[0],
         out_shape=pltpu.VMEM((4, WIDTH, 2 * LANES), jnp.float32),
         compiler_params=ROOM,
         name="terms",
-    )(joined, matrix)
+    )(place, own, other, matrix)
 
 
 def make_factor(gram):
@@ -208,7 +219,10 @@
     return inverse / half_across
 
 
-def last_kernel(parts_ref, columns_ref, joined_ref, matrix_ref, out_ref, done_ref, sems):
+def last_kernel(
+    place_ref, parts_ref, columns_ref, own_ref, other_ref, matrix_ref, out_ref, done_ref, sems
+):
+    held = (place_ref[0], own_ref, other_ref)
     total = (parts_ref[0] + parts_ref[1]) + (parts_ref[2] + parts_ref[3])
     factor = make_factor(total[:, LANES + WIDTH :])
     right = exact(factor, columns_ref[...], NN)
@@ -217,9 +231,9 @@
     high, low = split(jnp.concatenate([doubled(right), doubled(left)], axis=0))
     copies = []
     for unit in range(16):
-        rows = [reflector_block(joined_ref, unit, half) for half in range(2)]
+        rows = [reflector_block(*held, unit, half) for half in range(2)]
         rows = jnp.concatenate(rows, axis=0).T
-        left = split(jnp.concatenate([value_unit(joined_ref, unit), rows], axis=1))
+        left = split(jnp.concatenate([value_unit(*held, unit), rows], axis=1))
         change = dot(left[0], high, NN) + (dot(left[0], low, NN) + dot(left[1], high, NN))
         for half in range(2):
             start = (2 * unit + half) * LANES
@@ -234,10 +248,10 @@
         copy.wait()
 
 
-def last_step(parts, columns, joined, matrix):
+def last_step(place, parts, columns, own, other, matrix):
     return pl.pallas_call(
         last_kernel,
-        in_specs=in_vmem(4),
+        in_specs=[pl.BlockSpec(memory_space=pltpu.SMEM), *in_vmem(5)],
         out_specs=pl.BlockSpec(memory_space=pl.ANY),
         out_shape=jax.ShapeDtypeStruct(matrix.shape, jnp.float32),
         scratch_shapes=[
@@ -246,30 +260,33 @@
         ],
         compiler_params=ROOM,
         name="last",
-    )(parts, columns, joined, matrix)
+    )(place, parts, columns, own, other, matrix)
 
 
 def on_device(matrix, vectors):
-    width, piece = vectors.shape
+    width, span = vectors.shape
     core, x = lax.axis_index("core"), lax.axis_index("x")
-    masked = mask_vectors(vectors, lax.axis_index(("row", "zh", "zl")) * piece)
-    half = lax.dynamic_slice_in_dim(masked, core * LANES, LANES, 1)
-    columns = lax.ppermute(half, AXES, column_routes())
+    first = lax.axis_index(("zh", "zl", "x", "core")) * LANES
+    place = jnp.stack([core, first])
+    piece = lax.ppermute(vectors, AXES, column_routes())
+    masked = mask_vectors(vectors, lax.axis_index(("row", "zh", "zl")) * span)
     lines = lax.dynamic_slice_in_dim(masked, (core * 4 + x) * 8, 8, 0)
     lines = lines.reshape(8, 2, LANES).swapaxes(0, 1).reshape(16, LANES)
 
-    matrix, columns = staged(matrix), local(columns)
-    values = partial_value(columns, matrix)
+    matrix = staged(matrix)
+    values, columns = partial_value(place, piece, matrix)
     values = pair_summed(swapped(values.reshape(2, 16, WIDTH, LANES), "core"))
     values, lines = lax.optimization_barrier((values, lines))
     values = swapped(values, PLANE).sum(axis=0)
     far = shared(jnp.concatenate([values, lines], axis=0), "zh")
     summed = far[:, :WIDTH].sum(axis=0)
     own = jnp.concatenate([summed, far[:, WIDTH:].reshape(WIDTH, LANES)], axis=0)
-    joined = local(shared(shared(shared(own, "zl"), "x"), "core"))
-
-    parts = local(swapped(left_parts(joined, matrix), "row"))
-    return last_step(parts, columns, joined, matrix)
+    own = shared(shared(own, "zl"), "x")
+    other = local(lax.ppermute(own, "core", [(0, 1), (1, 0)]))
+    own = local(own)
+
+    parts = local(swapped(left_parts(place, own, other, matrix), "row"))
+    return last_step(place, parts, columns, own, other, matrix)
 
 
 def solution(mesh):

time: 120 us -> 125 us (1.042)
  starting transfers between devices: 5.65 us -> 14.6 us
  blocking collectives: 105 us -> 97 us
  waiting for transfers between devices: 0.01 us -> 2.27 us
  Pallas kernels: 7.82 us -> 9.52 us
    ppermute x1 -> x2, starting transfers between devices: 5.65 us -> 14.6 us  [the longest x1 8.92 us: on_device(): other = local(lax.ppermute(own, 'core', [(0, 1), (1, 0)]))]
    all_to_all x7 -> x6, blocking collectives: 105 us -> 97 us  [swapped(): return lax.all_to_all(array, axes, 0, 0, tiled=True)]
    ppermute x1 -> x2, waiting for transfers between devices: 0.01 us -> 2.27 us  [the longest x1 2.26 us: on_device(): other = local(lax.ppermute(own, 'core', [(0, 1), (1, 0)]))]
    pallas_call x3, Pallas kernels: 6.17 us -> 7.86 us  [the longest x1 4.13 us: last_step(): pl.pallas_call(last_kernel, in_specs=[pl.BlockSpec(memory_space=pltpu.SME...]
  transfers between devices with their start and end apart: 1 -> 2, of which waited for: 0 -> 1; matrix products, arithmetic and copies ran while one was open for 0% -> 1% of each run, Pallas kernels for 1% -> 1%
where the time goes in v7:
time: 125 us
  blocking collectives  97 us (78%)
  starting transfers between devices  14.6 us (12%)
  Pallas kernels  9.52 us (8%)
  waiting for transfers between devices  2.27 us (2%)
    all_to_all x6, blocking collectives, swapped(): return lax.all_to_all(array, axes, 0, 0, tiled=True)  97 us
    ppermute x1, starting transfers between devices, on_device(): other = local(lax.ppermute(own, 'core', [(0, 1), (1, 0)]))  8.92 us
    ppermute x1, starting transfers between devices, on_device(): piece = lax.ppermute(vectors, AXES, column_routes())  5.64 us
    pallas_call x1, Pallas kernels, last_step(): pl.pallas_call(last_kernel, in_specs=[pl.BlockSpec(memory_space=pltpu.SME...  4.13 us
  transfers between devices with their start and end apart: 2, of which 1 were waited for; matrix products, arithmetic and copies ran while one was open for 1% of the time, Pallas kernels for 1%

profile of v7, /device:TPU:1, one launch (start us, length us, event | category | flops | bytes accessed | tf_op | source)
XLA Modules:
  0.0 124.6 jit_solution(9996104978610787205)
XLA Ops:
  0.0 5.6 %collective-permute-start = (f32[64,256]{1,0:T(8,128)}, f32[64,256]{1,0:T(8,128)S(1)}, u32[]{:S(2)}, u32[]{:S(2)}) collective-permute-start(f32[64,256]{1,0:T(8,128)} %param.3), channel_id=1, source_target_pairs={{0,256},{1,257},{2,128},{3,129},{4,0},{5,1},{6,384},{7,385},{8,386... | collective-permute-start | bytes 196616 | tf_op jit(solution)/shard_map/ppermute | solution.py:271
  5.7 1.6 %staging.1.matrix_ref = f32[4096,128]{1,0:T(8,128)S(1)} custom-call(f32[4096,128]{1,0:T(8,128)} %matrix_ref.1), custom_call_target="tpu_custom_call" | custom-call | tf_op jit(solution)/shard_map/staging/pallas_call | solution.py:89
  7.3 0.1 dynamic-slice
  7.4 0.8 fusion
  8.2 0.1 pad_add_fusion.place_ref
  8.2 0.0 collective-permute-done.piece_ref
  8.2 1.5 %value.1 = (f32[32,64,128]{2,1,0:T(8,128)S(1)}, f32[64,128]{1,0:T(8,128)S(1)}) custom-call(s32[2]{0:T(128)S(1)} %pad_add_fusion.place_ref, f32[64,256]{1,0:T(8,128)S(1)} %collective-permute-done.piece_ref, f32[4096,128]{1,0:T(8,128)S(1)} %staging.1.matrix_ref), custom_call_target="tpu_custom_call" | custom-call | tf_op jit(solution)/shard_map/value/pallas_call | solution.py:131
  9.7 10.8 %all_to_all.30.pair_ref = f32[2,16,64,128]{3,2,1,0:T(8,128)S(1)} all-to-all(f32[2,16,64,128]{3,2,1,0:T(8,128)S(1)} %bitcast.10), channel_id=1, replica_groups=mesh['row'=4,'zh'=4,'zl'=4,'x'=4,'core'=2] {'core'}, dimensions={0} | all-to-all | bytes 2097152 | tf_op jit(solution)/shard_map/all_to_all | solution.py:38
  20.5 0.1 pair.1
  20.6 29.1 %all_to_all.31 = f32[16,64,128]{2,1,0:T(8,128)S(1)} all-to-all(f32[16,64,128]{2,1,0:T(8,128)S(1)} %pair.1), channel_id=1, replica_groups=mesh['row'=4,'zh'=4,'zl'=4,'x'=4,'core'=2] {'zl','x'}, dimensions={0} | all-to-all | bytes 1048576 | tf_op jit(solution)/shard_map/all_to_all | solution.py:38
  49.7 23.3 %all_to_all.32 = f32[4,80,128]{2,1,0:T(8,128)S(1)} all-to-all(f32[4,80,128]{2,1,0:T(8,128)S(1)} %broadcast_in_dim.21), channel_id=1, replica_groups=mesh['row'=4,'zh'=4,'zl'=4,'x'=4,'core'=2] {'zh'}, dimensions={0} | all-to-all | bytes 327680 | tf_op jit(solution)/shard_map/all_to_all | solution.py:38
  73.1 8.6 %all_to_all.33 = f32[4,128,128]{2,1,0:T(8,128)S(1)} all-to-all(f32[4,128,128]{2,1,0:T(8,128)S(1)} %broadcast_in_dim.22), channel_id=1, replica_groups=mesh['row'=4,'zh'=4,'zl'=4,'x'=4,'core'=2] {'zl'}, dimensions={0} | all-to-all | bytes 524288 | tf_op jit(solution)/shard_map/all_to_all | solution.py:38
  81.7 0.1 broadcast_in_dim.23
  81.8 12.4 %all_to_all.34.own_ref = f32[4,4,128,128]{3,2,1,0:T(8,128)S(1)} all-to-all(f32[4,4,128,128]{3,2,1,0:T(8,128)S(1)} %broadcast_in_dim.23), channel_id=1, replica_groups=mesh['row'=4,'zh'=4,'zl'=4,'x'=4,'core'=2] {'x'}, dimensions={0} | all-to-all | bytes 2097152 | tf_op jit(solution)/shard_map/all_to_all | solution.py:38
  94.2 8.9 %collective-permute-start.1 = (f32[4,4,128,128]{3,2,1,0:T(8,128)S(1)}, f32[4,4,128,128]{3,2,1,0:T(8,128)S(1)}, u32[]{:S(2)}, u32[]{:S(2)}) collective-permute-start(f32[4,4,128,128]{3,2,1,0:T(8,128)S(1)} %all_to_all.34.own_ref), channel_id=1, source_target_pairs={{0,1},{1,0},{2,3},{3,2},{4,5},{5,4},{6,7},{7,6},{8,9},{9,8},{10,11... | collective-permute-start | bytes 3145736 | tf_op jit(solution)/shard_map/ppermute | solution.py:285
  103.2 2.3 %collective-permute-done.1.other_ref = f32[4,4,128,128]{3,2,1,0:T(8,128)S(1)} collective-permute-done((f32[4,4,128,128]{3,2,1,0:T(8,128)S(1)}, f32[4,4,128,128]{3,2,1,0:T(8,128)S(1)}, u32[]{:S(2)}, u32[]{:S(2)}) %collective-permute-start.1) | collective-permute-done | bytes 1048608 | tf_op jit(solution)/shard_map/ppermute | solution.py:285
  105.4 2.3 %terms.1 = f32[4,64,256]{2,1,0:T(8,128)S(1)} custom-call(s32[2]{0:T(128)S(1)} %pad_add_fusion.place_ref, f32[4,4,128,128]{3,2,1,0:T(8,128)S(1)} %all_to_all.34.own_ref, f32[4,4,128,128]{3,2,1,0:T(8,128)S(1)} %collective-permute-done.1.other_ref, f32[4096,128]{1,0:T(8,128)S(1)} %staging.1.matrix_ref), custom_call_target="tpu_custom_call" | custom-call | tf_op jit(solution)/shard_map/terms/pallas_call | solution.py:195
  107.7 12.7 %all_to_all.35.parts_ref = f32[4,64,256]{2,1,0:T(8,128)S(1)} all-to-all(f32[4,64,256]{2,1,0:T(8,128)S(1)} %terms.1), channel_id=1, replica_groups=mesh['row'=4,'zh'=4,'zl'=4,'x'=4,'core'=2] {'row'}, dimensions={0} | all-to-all | bytes 524288 | tf_op jit(solution)/shard_map/all_to_all | solution.py:38
  120.5 4.1 %last.1 = f32[4096,128]{1,0:T(8,128)} custom-call(s32[2]{0:T(128)S(1)} %pad_add_fusion.place_ref, f32[4,64,256]{2,1,0:T(8,128)S(1)} %all_to_all.35.parts_ref, f32[64,128]{1,0:T(8,128)S(1)} %get-tuple-element.12.columns_ref, f32[4,4,128,128]{3,2,1,0:T(8,128)S(1)} %all_to_all.34.own_ref, f32[4,4,128,128]{3,2,1,0:T(8,128)S(1)} %collective-permute-done.1.other_ref, ...), custom_call_target="tpu_custom_call" | custom-call | tf_op jit(solution)/shard_map/last/pallas_call | solution.py:252
  (9 shorter events, 0.1 us)
Async XLA Ops:
  0.0 8.2 %collective-permute-start = (f32[64,256]{1,0:T(8,128)}, f32[64,256]{1,0:T(8,128)S(1)}, u32[]{:S(2)}, u32[]{:S(2)}) collective-permute-start(f32[64,256]{1,0:T(8,128)} %param.3), channel_id=1, source_target_pairs={{0,256},{1,257},{2,128},{3,129},{4,0},{5,1},{6,384},{7,385},{8,386... | collective-permute-start | bytes 196616 | tf_op jit(solution)/shard_map/ppermute | solution.py:271
  94.2 11.2 %collective-permute-start.1 = (f32[4,4,128,128]{3,2,1,0:T(8,128)S(1)}, f32[4,4,128,128]{3,2,1,0:T(8,128)S(1)}, u32[]{:S(2)}, u32[]{:S(2)}) collective-permute-start(f32[4,4,128,128]{3,2,1,0:T(8,128)S(1)} %all_to_all.34.own_ref), channel_id=1, source_target_pairs={{0,1},{1,0},{2,3},{3,2},{4,5},{5,4},{6,7},{7,6},{8,9},{9,8},{10,11... | collective-permute-start | bytes 3145736 | tf_op jit(solution)/shard_map/ppermute | solution.py:285

commit v8 on v4

--- a/solution.py
+++ b/solution.py
@@ -135,16 +135,20 @@
     )(columns, matrix)
 
 
-def reflector_block(joined_ref, unit, half):
+def reflector_block(flag_ref, own_ref, other_ref, unit, half):
     zh, zl = divmod(unit, 4)
     start = WIDTH + zh * 16 + half * 8
-    return joined_ref[:, :, zl, start : start + 8, :].reshape(WIDTH, LANES)
-
-
-def value_unit(joined_ref, unit):
-    piece = 2 * unit
-    core, zl, x = piece // 16, piece // 4 % 4, piece % 4
-    return joined_ref[core, x : x + 2, zl, :WIDTH, :].reshape(2 * WIDTH, LANES)
+    own, other = own_ref[:, zl, start : start + 8, :], other_ref[:, zl, start : start + 8, :]
+    first = flag_ref[...] == 0
+    rows = [jnp.where(first, own, other), jnp.where(first, other, own)]
+    return jnp.concatenate(rows, axis=0).reshape(WIDTH, LANES)
+
+
+def value_unit(flag_ref, own_ref, other_ref, unit):
+    core, zl, x = unit // 8, unit // 2 % 4, 2 * unit % 4
+    own, other = own_ref[x : x + 2, zl, :WIDTH, :], other_ref[x : x + 2, zl, :WIDTH, :]
+    own, other = own.reshape(16, 8, LANES), other.reshape(16, 8, LANES)
+    return jnp.where(flag_ref[...] == core, own, other).reshape(2 * WIDTH, LANES)
 
 
 def in_three(array):
@@ -153,17 +157,18 @@
     return jnp.concatenate([high, low, rest.astype(jnp.bfloat16)], axis=0)
 
 
-def terms_kernel(joined_ref, matrix_ref, out_ref):
+def terms_kernel(flag_ref, own_ref, other_ref, matrix_ref, out_ref):
+    held = (flag_ref, own_ref, other_ref)
     plain = jnp.zeros((2 * WIDTH, 2 * LANES), jnp.float32)
     cross = jnp.zeros((4 * WIDTH, 2 * LANES), jnp.float32)
     gram = jnp.zeros((3 * WIDTH, 3 * WIDTH), jnp.float32)
     for unit in range(16):
-        rows = [reflector_block(joined_ref, unit, half) for half in range(2)]
+        rows = [reflector_block(*held, unit, half) for half in range(2)]
         rows = in_three(jnp.concatenate(rows, axis=1))
         span = slice(2 * unit * LANES, 2 * (unit + 1) * LANES)
         right = jnp.concatenate(split(matrix_ref[span, :]), axis=1)
         plain += dot(rows[: 2 * WIDTH], right, NN)
-        right = jnp.concatenate(split(value_unit(joined_ref, unit)), axis=1)
+        right = jnp.concatenate(split(value_unit(*held, unit)), axis=1)
         both = [rows[: 2 * WIDTH, :LANES], rows[: 2 * WIDTH, LANES:]]
         cross += dot(jnp.concatenate(both, axis=0), right, NN)
         gram += dot(rows, rows, NT)
@@ -180,15 +185,15 @@
         out_ref[y] = joined
 
 
-def left_parts(joined, matrix):
+def left_parts(held, matrix):
     return pl.pallas_call(
         terms_kernel,
-        in_specs=in_vmem(2),
+        in_specs=in_vmem(4),
         out_specs=in_vmem(1)[0],
         out_shape=pltpu.VMEM((4, WIDTH, 2 * LANES), jnp.float32),
         compiler_params=ROOM,
         name="terms",
-    )(joined, matrix)
+    )(*held, matrix)
 
 
 def make_factor(gram):
@@ -208,7 +213,10 @@
     return inverse / half_across
 
 
-def last_kernel(parts_ref, columns_ref, joined_ref, matrix_ref, out_ref, done_ref, sems):
+def last_kernel(
+    parts_ref, columns_ref, flag_ref, own_ref, other_ref, matrix_ref, out_ref, done_ref, sems
+):
+    held = (flag_ref, own_ref, other_ref)
     total = (parts_ref[0] + parts_ref[1]) + (parts_ref[2] + parts_ref[3])
     factor = make_factor(total[:, LANES + WIDTH :])
     right = exact(factor, columns_ref[...], NN)
@@ -217,9 +225,9 @@
     high, low = split(jnp.concatenate([doubled(right), doubled(left)], axis=0))
     copies = []
     for unit in range(16):
-        rows = [reflector_block(joined_ref, unit, half) for half in range(2)]
+        rows = [reflector_block(*held, unit, half) for half in range(2)]
         rows = jnp.concatenate(rows, axis=0).T
-        left = split(jnp.concatenate([value_unit(joined_ref, unit), rows], axis=1))
+        left = split(jnp.concatenate([value_unit(*held, unit), rows], axis=1))
         change = dot(left[0], high, NN) + (dot(left[0], low, NN) + dot(left[1], high, NN))
         for half in range(2):
             start = (2 * unit + half) * LANES
@@ -234,10 +242,10 @@
         copy.wait()
 
 
-def last_step(parts, columns, joined, matrix):
+def last_step(parts, columns, held, matrix):
     return pl.pallas_call(
         last_kernel,
-        in_specs=in_vmem(4),
+        in_specs=in_vmem(6),
         out_specs=pl.BlockSpec(memory_space=pl.ANY),
         out_shape=jax.ShapeDtypeStruct(matrix.shape, jnp.float32),
         scratch_shapes=[
@@ -246,7 +254,7 @@
         ],
         compiler_params=ROOM,
         name="last",
-    )(parts, columns, joined, matrix)
+    )(parts, columns, *held, matrix)
 
 
 def on_device(matrix, vectors):
@@ -261,15 +269,18 @@
     matrix, columns = staged(matrix), local(columns)
     values = partial_value(columns, matrix)
     values = pair_summed(swapped(values.reshape(2, 16, WIDTH, LANES), "core"))
-    values, lines = lax.optimization_barrier((values, lines))
+    flag = jnp.full((8, LANES), core, jnp.int32)
+    values, lines, flag = lax.optimization_barrier((values, lines, flag))
     values = swapped(values, PLANE).sum(axis=0)
     far = shared(jnp.concatenate([values, lines], axis=0), "zh")
     summed = far[:, :WIDTH].sum(axis=0)
     own = jnp.concatenate([summed, far[:, WIDTH:].reshape(WIDTH, LANES)], axis=0)
-    joined = local(shared(shared(shared(own, "zl"), "x"), "core"))
-
-    parts = local(swapped(left_parts(joined, matrix), "row"))
-    return last_step(parts, columns, joined, matrix)
+    own = shared(shared(own, "zl"), "x")
+    other = lax.ppermute(own, "core", [(0, 1), (1, 0)])
+    held = (local(flag), local(own), local(other))
+
+    parts = local(swapped(left_parts(held, matrix), "row"))
+    return last_step(parts, columns, held, matrix)
 
 
 def solution(mesh):

time: 120 us -> 119 us (level)
  blocking collectives: 105 us -> 94.4 us
  starting transfers between devices: 5.65 us -> 13 us
  waiting for transfers between devices: 0.01 us -> 2.27 us
    all_to_all x7 -> x6, blocking collectives: 105 us -> 94.4 us  [swapped(): return lax.all_to_all(array, axes, 0, 0, tiled=True)]
    ppermute x0 -> x1, starting transfers between devices: none -> 7.32 us  [on_device(): other = lax.ppermute(own, 'core', [(0, 1), (1, 0)])]
    ppermute x0 -> x1, waiting for transfers between devices: none -> 2.26 us  [on_device(): other = lax.ppermute(own, 'core', [(0, 1), (1, 0)])]
  transfers between devices with their start and end apart: 1 -> 2, of which waited for: 0 -> 1; matrix products, arithmetic and copies ran while one was open for 0% -> 0% of each run, Pallas kernels for 1% -> 1%
where the time goes in v8:
time: 119 us
  blocking collectives  94.4 us (79%)
  starting transfers between devices  13 us (11%)
  Pallas kernels  7.82 us (7%)
  waiting for transfers between devices  2.27 us (2%)
    all_to_all x6, blocking collectives, swapped(): return lax.all_to_all(array, axes, 0, 0, tiled=True)  94.4 us
    ppermute x1, starting transfers between devices, on_device(): other = lax.ppermute(own, 'core', [(0, 1), (1, 0)])  7.32 us
    ppermute x1, starting transfers between devices, on_device(): columns = lax.ppermute(half, AXES, column_routes())  5.65 us
    pallas_call x1, Pallas kernels, last_step(): pl.pallas_call(last_kernel, in_specs=in_vmem(6), out_specs=pl.BlockSpec(m...  3.6 us
  transfers between devices with their start and end apart: 2, of which 1 were waited for; matrix products, arithmetic and copies ran while one was open for 0% of the time, Pallas kernels for 1%

profile of v8, /device:TPU:1, one launch (start us, length us, event | category | flops | bytes accessed | tf_op | source)
XLA Modules:
  0.0 118.7 jit_solution(10203622435013125403)
XLA Ops:
  0.0 0.9 select_select_fusion
  1.0 5.7 %collective-permute-start = (f32[64,128]{1,0:T(8,128)S(1)}, f32[64,128]{1,0:T(8,128)S(1)}, u32[]{:S(2)}, u32[]{:S(2)}) collective-permute-start(f32[64,128]{1,0:T(8,128)S(1)} %constant_dynamic-slice_fusion), channel_id=1, source_target_pairs={{0,256},{1,257},{2,128},{3,129},{4,0},{5,1},{6,384},{7,385},{8,386... | collective-permute-start | bytes 98312 | tf_op jit(solution)/shard_map/ppermute | solution.py:265
  6.6 1.6 %staging.1.matrix_ref = f32[4096,128]{1,0:T(8,128)S(1)} custom-call(f32[4096,128]{1,0:T(8,128)} %matrix_ref.1), custom_call_target="tpu_custom_call" | custom-call | tf_op jit(solution)/shard_map/staging/pallas_call | solution.py:89
  8.2 0.0 collective-permute-done.columns_ref
  8.3 0.9 value.1
  9.1 11.1 %all_to_all.30.pair_ref = f32[2,16,64,128]{3,2,1,0:T(8,128)S(1)} all-to-all(f32[2,16,64,128]{3,2,1,0:T(8,128)S(1)} %bitcast.8), channel_id=1, replica_groups=mesh['row'=4,'zh'=4,'zl'=4,'x'=4,'core'=2] {'core'}, dimensions={0} | all-to-all | bytes 2097152 | tf_op jit(solution)/shard_map/all_to_all | solution.py:38
  20.2 0.1 pair.1
  20.3 25.3 %all_to_all.31 = f32[16,64,128]{2,1,0:T(8,128)S(1)} all-to-all(f32[16,64,128]{2,1,0:T(8,128)S(1)} %pair.1), channel_id=1, replica_groups=mesh['row'=4,'zh'=4,'zl'=4,'x'=4,'core'=2] {'zl','x'}, dimensions={0} | all-to-all | bytes 1048576 | tf_op jit(solution)/shard_map/all_to_all | solution.py:38
  45.7 24.7 %all_to_all.32 = f32[4,80,128]{2,1,0:T(8,128)S(1)} all-to-all(f32[4,80,128]{2,1,0:T(8,128)S(1)} %broadcast_in_dim.25), channel_id=1, replica_groups=mesh['row'=4,'zh'=4,'zl'=4,'x'=4,'core'=2] {'zh'}, dimensions={0} | all-to-all | bytes 327680 | tf_op jit(solution)/shard_map/all_to_all | solution.py:38
  70.4 10.4 %all_to_all.33 = f32[4,128,128]{2,1,0:T(8,128)S(1)} all-to-all(f32[4,128,128]{2,1,0:T(8,128)S(1)} %broadcast_in_dim.26), channel_id=1, replica_groups=mesh['row'=4,'zh'=4,'zl'=4,'x'=4,'core'=2] {'zl'}, dimensions={0} | all-to-all | bytes 524288 | tf_op jit(solution)/shard_map/all_to_all | solution.py:38
  80.9 0.1 broadcast_in_dim.27
  81.0 13.0 %all_to_all.34.own_ref = f32[4,4,128,128]{3,2,1,0:T(8,128)S(1)} all-to-all(f32[4,4,128,128]{3,2,1,0:T(8,128)S(1)} %broadcast_in_dim.27), channel_id=1, replica_groups=mesh['row'=4,'zh'=4,'zl'=4,'x'=4,'core'=2] {'x'}, dimensions={0} | all-to-all | bytes 2097152 | tf_op jit(solution)/shard_map/all_to_all | solution.py:38
  94.0 7.3 %collective-permute-start.1 = (f32[4,4,128,128]{3,2,1,0:T(8,128)S(1)}, f32[4,4,128,128]{3,2,1,0:T(8,128)S(1)}, u32[]{:S(2)}, u32[]{:S(2)}) collective-permute-start(f32[4,4,128,128]{3,2,1,0:T(8,128)S(1)} %all_to_all.34.own_ref), channel_id=1, source_target_pairs={{0,1},{1,0},{2,3},{3,2},{4,5},{5,4},{6,7},{7,6},{8,9},{9,8},{10,11... | collective-permute-start | bytes 3145736 | tf_op jit(solution)/shard_map/ppermute | solution.py:279
  101.3 2.3 %collective-permute-done.1.other_ref = f32[4,4,128,128]{3,2,1,0:T(8,128)S(1)} collective-permute-done((f32[4,4,128,128]{3,2,1,0:T(8,128)S(1)}, f32[4,4,128,128]{3,2,1,0:T(8,128)S(1)}, u32[]{:S(2)}, u32[]{:S(2)}) %collective-permute-start.1) | collective-permute-done | bytes 1048608 | tf_op jit(solution)/shard_map/ppermute | solution.py:279
  103.6 1.7 %terms.1 = f32[4,64,256]{2,1,0:T(8,128)S(1)} custom-call(s32[8,128]{1,0:T(8,128)S(1)} %broadcast_in_dim.24.flag_ref, f32[4,4,128,128]{3,2,1,0:T(8,128)S(1)} %all_to_all.34.own_ref, f32[4,4,128,128]{3,2,1,0:T(8,128)S(1)} %collective-permute-done.1.other_ref, f32[4096,128]{1,0:T(8,128)S(1)} %staging.1.matrix_ref), custom_call_target="tpu_custom_call" | custom-call | tf_op jit(solution)/shard_map/terms/pallas_call | solution.py:189
  105.3 9.8 %all_to_all.35.parts_ref = f32[4,64,256]{2,1,0:T(8,128)S(1)} all-to-all(f32[4,64,256]{2,1,0:T(8,128)S(1)} %terms.1), channel_id=1, replica_groups=mesh['row'=4,'zh'=4,'zl'=4,'x'=4,'core'=2] {'row'}, dimensions={0} | all-to-all | bytes 524288 | tf_op jit(solution)/shard_map/all_to_all | solution.py:38
  115.1 3.6 %last.1 = f32[4096,128]{1,0:T(8,128)} custom-call(f32[4,64,256]{2,1,0:T(8,128)S(1)} %all_to_all.35.parts_ref, f32[64,128]{1,0:T(8,128)S(1)} %collective-permute-done.columns_ref, s32[8,128]{1,0:T(8,128)S(1)} %broadcast_in_dim.24.flag_ref, f32[4,4,128,128]{3,2,1,0:T(8,128)S(1)} %all_to_all.34.own_ref, ...), custom_call_target="tpu_custom_call" | custom-call | tf_op jit(solution)/shard_map/last/pallas_call | solution.py:246
  (12 shorter events, 0.1 us)
Async XLA Ops:
  1.0 7.3 %collective-permute-start = (f32[64,128]{1,0:T(8,128)S(1)}, f32[64,128]{1,0:T(8,128)S(1)}, u32[]{:S(2)}, u32[]{:S(2)}) collective-permute-start(f32[64,128]{1,0:T(8,128)S(1)} %constant_dynamic-slice_fusion), channel_id=1, source_target_pairs={{0,256},{1,257},{2,128},{3,129},{4,0},{5,1},{6,384},{7,385},{8,386... | collective-permute-start | bytes 98312 | tf_op jit(solution)/shard_map/ppermute | solution.py:265
  94.0 9.6 %collective-permute-start.1 = (f32[4,4,128,128]{3,2,1,0:T(8,128)S(1)}, f32[4,4,128,128]{3,2,1,0:T(8,128)S(1)}, u32[]{:S(2)}, u32[]{:S(2)}) collective-permute-start(f32[4,4,128,128]{3,2,1,0:T(8,128)S(1)} %all_to_all.34.own_ref), channel_id=1, source_target_pairs={{0,1},{1,0},{2,3},{3,2},{4,5},{5,4},{6,7},{7,6},{8,9},{9,8},{10,11... | collective-permute-start | bytes 3145736 | tf_op jit(solution)/shard_map/ppermute | solution.py:279

commit v9 on v8

--- a/solution.py
+++ b/solution.py
@@ -97,42 +97,49 @@
     )(pltpu.with_memory_space_constraint(matrix, pltpu.HBM))
 
 
-def pair_kernel(pair_ref, out_ref):
-    out_ref[...] = pair_ref[0] + pair_ref[1]
-
-
-def pair_summed(pair):
+def pair_kernel(kept_ref, sent_ref, out_ref):
+    out_ref[...] = kept_ref[...] + sent_ref[...]
+
+
+def pair_summed(kept, sent):
     return pl.pallas_call(
         pair_kernel,
-        in_specs=in_vmem(1),
+        in_specs=in_vmem(2),
         out_specs=in_vmem(1)[0],
-        out_shape=pltpu.VMEM(pair.shape[1:], jnp.float32),
+        out_shape=pltpu.VMEM(kept.shape, jnp.float32),
         compiler_params=ROOM,
         name="pair",
-    )(local(pair))
-
-
-def value_kernel(columns_ref, matrix_ref, out_ref):
+    )(kept, local(sent))
+
+
+def value_kernel(flag_ref, columns_ref, matrix_ref, keep_ref, send_ref):
     high, low = split(doubled(columns_ref[...].T))
     right = jnp.concatenate([high, low], axis=1)
-    for unit in range(16):
-        first = matrix_ref[2 * unit * LANES : (2 * unit + 1) * LANES, :]
-        second = matrix_ref[(2 * unit + 1) * LANES : (2 * unit + 2) * LANES, :]
-        high, low = split(jnp.concatenate([first, second], axis=1))
-        both = dot(high, right, NN) + dot(low, right, NN)
-        total = both[:, :LANES] + both[:, LANES:]
-        out_ref[2 * unit : 2 * unit + 2] = total.reshape(2, WIDTH, LANES)
-
-
-def partial_value(columns, matrix):
+    first = flag_ref[...] == 0
+    for unit in range(8):
+        low, high = [value_rows(matrix_ref, right, k) for k in (unit, unit + 8)]
+        span = slice(2 * unit, 2 * unit + 2)
+        keep_ref[span] = jnp.where(first, low, high).reshape(2, WIDTH, LANES)
+        send_ref[span] = jnp.where(first, high, low).reshape(2, WIDTH, LANES)
+
+
+def value_rows(matrix_ref, right, unit):
+    first = matrix_ref[2 * unit * LANES : (2 * unit + 1) * LANES, :]
+    second = matrix_ref[(2 * unit + 1) * LANES : (2 * unit + 2) * LANES, :]
+    high, low = split(jnp.concatenate([first, second], axis=1))
+    both = dot(high, right, NN) + dot(low, right, NN)
+    return (both[:, :LANES] + both[:, LANES:]).reshape(16, 8, LANES)
+
+
+def partial_value(flag, columns, matrix):
     return pl.pallas_call(
         value_kernel,
-        in_specs=in_vmem(2),
-        out_specs=in_vmem(1)[0],
-        out_shape=pltpu.VMEM((32, WIDTH, LANES), jnp.float32),
+        in_specs=in_vmem(3),
+        out_specs=in_vmem(2),
+        out_shape=[pltpu.VMEM((16, WIDTH, LANES), jnp.float32)] * 2,
         compiler_params=ROOM,
         name="value",
-    )(columns, matrix)
+    )(flag, columns, matrix)
 
 
 def reflector_block(flag_ref, own_ref, other_ref, unit, half):
@@ -267,9 +274,9 @@
     lines = lines.reshape(8, 2, LANES).swapaxes(0, 1).reshape(16, LANES)
 
     matrix, columns = staged(matrix), local(columns)
-    values = partial_value(columns, matrix)
-    values = pair_summed(swapped(values.reshape(2, 16, WIDTH, LANES), "core"))
     flag = jnp.full((8, LANES), core, jnp.int32)
+    kept, sent = partial_value(local(flag), columns, matrix)
+    values = pair_summed(kept, lax.ppermute(local(sent), "core", [(0, 1), (1, 0)]))
     values, lines, flag = lax.optimization_barrier((values, lines, flag))
     values = swapped(values, PLANE).sum(axis=0)
     far = shared(jnp.concatenate([values, lines], axis=0), "zh")

time: 119 us -> 119 us (level)
  blocking collectives: 94.4 us -> 83.3 us
  starting transfers between devices: 13 us -> 21.8 us
  waiting for transfers between devices: 2.27 us -> 3.97 us
    all_to_all x6 -> x5, blocking collectives: 94.4 us -> 83.3 us  [swapped(): return lax.all_to_all(array, axes, 0, 0, tiled=True)]
    ppermute x0 -> x1, starting transfers between devices: none -> 8.8 us  [on_device(): lax.ppermute(local(sent), 'core', [(0, 1), (1, 0)])]
    ppermute x0 -> x1, waiting for transfers between devices: none -> 1.7 us  [on_device(): lax.ppermute(local(sent), 'core', [(0, 1), (1, 0)])]
  transfers between devices with their start and end apart: 2 -> 3, of which waited for: 1 -> 2; matrix products, arithmetic and copies ran while one was open for 0% -> 0% of each run, Pallas kernels for 1% -> 1%
where the time goes in v9:
time: 119 us
  blocking collectives  83.3 us (70%)
  starting transfers between devices  21.8 us (18%)
  Pallas kernels  8.62 us (7%)
  waiting for transfers between devices  3.97 us (3%)
    all_to_all x5, blocking collectives, swapped(): return lax.all_to_all(array, axes, 0, 0, tiled=True)  83.3 us
    ppermute x1, starting transfers between devices, on_device(): lax.ppermute(local(sent), 'core', [(0, 1), (1, 0)])  8.8 us
    ppermute x1, starting transfers between devices, on_device(): other = lax.ppermute(own, 'core', [(0, 1), (1, 0)])  7.32 us
    ppermute x1, starting transfers between devices, on_device(): columns = lax.ppermute(half, AXES, column_routes())  5.65 us
    pallas_call x1, Pallas kernels, last_step(): pl.pallas_call(last_kernel, in_specs=in_vmem(6), out_specs=pl.BlockSpec(m...  3.6 us
  transfers between devices with their start and end apart: 3, of which 2 were waited for; matrix products, arithmetic and copies ran while one was open for 0% of the time, Pallas kernels for 1%

profile of v9, /device:TPU:1, one launch (start us, length us, event | category | flops | bytes accessed | tf_op | source)
XLA Modules:
  0.0 118.9 jit_solution(8670175091485709930)
XLA Ops:
  0.0 0.9 select_select_fusion
  1.0 5.7 %collective-permute-start = (f32[64,128]{1,0:T(8,128)S(1)}, f32[64,128]{1,0:T(8,128)S(1)}, u32[]{:S(2)}, u32[]{:S(2)}) collective-permute-start(f32[64,128]{1,0:T(8,128)S(1)} %constant_dynamic-slice_fusion), channel_id=1, source_target_pairs={{0,256},{1,257},{2,128},{3,129},{4,0},{5,1},{6,384},{7,385},{8,386... | collective-permute-start | bytes 98312 | tf_op jit(solution)/shard_map/ppermute | solution.py:272
  6.6 1.6 %staging.1.matrix_ref = f32[4096,128]{1,0:T(8,128)S(1)} custom-call(f32[4096,128]{1,0:T(8,128)} %matrix_ref.1), custom_call_target="tpu_custom_call" | custom-call | tf_op jit(solution)/shard_map/staging/pallas_call | solution.py:89
  8.2 0.0 collective-permute-done.columns_ref
  8.2 1.7 %value.1 = (f32[16,64,128]{2,1,0:T(8,128)S(1)}, f32[16,64,128]{2,1,0:T(8,128)}) custom-call(s32[8,128]{1,0:T(8,128)S(1)} %broadcast_in_dim.22.flag_ref, f32[64,128]{1,0:T(8,128)S(1)} %collective-permute-done.columns_ref, f32[4096,128]{1,0:T(8,128)S(1)} %staging.1.matrix_ref), custom_call_target="tpu_custom_call" | custom-call | tf_op jit(solution)/shard_map/value/pallas_call | solution.py:135
  9.9 8.8 %collective-permute-start.1 = (f32[16,64,128]{2,1,0:T(8,128)}, f32[16,64,128]{2,1,0:T(8,128)S(1)}, u32[]{:S(2)}, u32[]{:S(2)}) collective-permute-start(f32[16,64,128]{2,1,0:T(8,128)} %get-tuple-element.11), channel_id=1, source_target_pairs={{0,1},{1,0},{2,3},{3,2},{4,5},{5,4},{6,7},{7,6},{8,9},{9,8},{10,11... | collective-permute-start | bytes 1572872 | tf_op jit(solution)/shard_map/ppermute | solution.py:279
  18.7 1.7 %collective-permute-done.1.sent_ref = f32[16,64,128]{2,1,0:T(8,128)S(1)} collective-permute-done((f32[16,64,128]{2,1,0:T(8,128)}, f32[16,64,128]{2,1,0:T(8,128)S(1)}, u32[]{:S(2)}, u32[]{:S(2)}) %collective-permute-start.1) | collective-permute-done | bytes 524320 | tf_op jit(solution)/shard_map/ppermute | solution.py:279
  20.4 0.1 pair.1
  20.5 25.3 %all_to_all.25 = f32[16,64,128]{2,1,0:T(8,128)S(1)} all-to-all(f32[16,64,128]{2,1,0:T(8,128)S(1)} %pair.1), channel_id=1, replica_groups=mesh['row'=4,'zh'=4,'zl'=4,'x'=4,'core'=2] {'zl','x'}, dimensions={0} | all-to-all | bytes 1048576 | tf_op jit(solution)/shard_map/all_to_all | solution.py:38
  45.9 24.7 %all_to_all.26 = f32[4,80,128]{2,1,0:T(8,128)S(1)} all-to-all(f32[4,80,128]{2,1,0:T(8,128)S(1)} %broadcast_in_dim.25), channel_id=1, replica_groups=mesh['row'=4,'zh'=4,'zl'=4,'x'=4,'core'=2] {'zh'}, dimensions={0} | all-to-all | bytes 327680 | tf_op jit(solution)/shard_map/all_to_all | solution.py:38
  70.7 10.4 %all_to_all.27 = f32[4,128,128]{2,1,0:T(8,128)S(1)} all-to-all(f32[4,128,128]{2,1,0:T(8,128)S(1)} %broadcast_in_dim.26), channel_id=1, replica_groups=mesh['row'=4,'zh'=4,'zl'=4,'x'=4,'core'=2] {'zl'}, dimensions={0} | all-to-all | bytes 524288 | tf_op jit(solution)/shard_map/all_to_all | solution.py:38
  81.1 0.1 broadcast_in_dim.27
  81.2 13.0 %all_to_all.28.own_ref = f32[4,4,128,128]{3,2,1,0:T(8,128)S(1)} all-to-all(f32[4,4,128,128]{3,2,1,0:T(8,128)S(1)} %broadcast_in_dim.27), channel_id=1, replica_groups=mesh['row'=4,'zh'=4,'zl'=4,'x'=4,'core'=2] {'x'}, dimensions={0} | all-to-all | bytes 2097152 | tf_op jit(solution)/shard_map/all_to_all | solution.py:38
  94.2 7.3 %collective-permute-start.2 = (f32[4,4,128,128]{3,2,1,0:T(8,128)S(1)}, f32[4,4,128,128]{3,2,1,0:T(8,128)S(1)}, u32[]{:S(2)}, u32[]{:S(2)}) collective-permute-start(f32[4,4,128,128]{3,2,1,0:T(8,128)S(1)} %all_to_all.28.own_ref), channel_id=1, source_target_pairs={{0,1},{1,0},{2,3},{3,2},{4,5},{5,4},{6,7},{7,6},{8,9},{9,8},{10,11... | collective-permute-start | bytes 3145736 | tf_op jit(solution)/shard_map/ppermute | solution.py:286
  101.6 2.3 %collective-permute-done.2.other_ref = f32[4,4,128,128]{3,2,1,0:T(8,128)S(1)} collective-permute-done((f32[4,4,128,128]{3,2,1,0:T(8,128)S(1)}, f32[4,4,128,128]{3,2,1,0:T(8,128)S(1)}, u32[]{:S(2)}, u32[]{:S(2)}) %collective-permute-start.2) | collective-permute-done | bytes 1048608 | tf_op jit(solution)/shard_map/ppermute | solution.py:286
  103.8 1.7 %terms.1 = f32[4,64,256]{2,1,0:T(8,128)S(1)} custom-call(s32[8,128]{1,0:T(8,128)S(1)} %broadcast_in_dim.22.flag_ref, f32[4,4,128,128]{3,2,1,0:T(8,128)S(1)} %all_to_all.28.own_ref, f32[4,4,128,128]{3,2,1,0:T(8,128)S(1)} %collective-permute-done.2.other_ref, f32[4096,128]{1,0:T(8,128)S(1)} %staging.1.matrix_ref), custom_call_target="tpu_custom_call" | custom-call | tf_op jit(solution)/shard_map/terms/pallas_call | solution.py:196
  105.5 9.8 %all_to_all.29.parts_ref = f32[4,64,256]{2,1,0:T(8,128)S(1)} all-to-all(f32[4,64,256]{2,1,0:T(8,128)S(1)} %terms.1), channel_id=1, replica_groups=mesh['row'=4,'zh'=4,'zl'=4,'x'=4,'core'=2] {'row'}, dimensions={0} | all-to-all | bytes 524288 | tf_op jit(solution)/shard_map/all_to_all | solution.py:38
  115.3 3.6 %last.1 = f32[4096,128]{1,0:T(8,128)} custom-call(f32[4,64,256]{2,1,0:T(8,128)S(1)} %all_to_all.29.parts_ref, f32[64,128]{1,0:T(8,128)S(1)} %collective-permute-done.columns_ref, s32[8,128]{1,0:T(8,128)S(1)} %broadcast_in_dim.22.flag_ref, f32[4,4,128,128]{3,2,1,0:T(8,128)S(1)} %all_to_all.28.own_ref, ...), custom_call_target="tpu_custom_call" | custom-call | tf_op jit(solution)/shard_map/last/pallas_call | solution.py:253
  (12 shorter events, 0.1 us)
Async XLA Ops:
  1.0 7.3 %collective-permute-start = (f32[64,128]{1,0:T(8,128)S(1)}, f32[64,128]{1,0:T(8,128)S(1)}, u32[]{:S(2)}, u32[]{:S(2)}) collective-permute-start(f32[64,128]{1,0:T(8,128)S(1)} %constant_dynamic-slice_fusion), channel_id=1, source_target_pairs={{0,256},{1,257},{2,128},{3,129},{4,0},{5,1},{6,384},{7,385},{8,386... | collective-permute-start | bytes 98312 | tf_op jit(solution)/shard_map/ppermute | solution.py:272
  9.9 10.5 %collective-permute-start.1 = (f32[16,64,128]{2,1,0:T(8,128)}, f32[16,64,128]{2,1,0:T(8,128)S(1)}, u32[]{:S(2)}, u32[]{:S(2)}) collective-permute-start(f32[16,64,128]{2,1,0:T(8,128)} %get-tuple-element.11), channel_id=1, source_target_pairs={{0,1},{1,0},{2,3},{3,2},{4,5},{5,4},{6,7},{7,6},{8,9},{9,8},{10,11... | collective-permute-start | bytes 1572872 | tf_op jit(solution)/shard_map/ppermute | solution.py:279
  94.2 9.6 %collective-permute-start.2 = (f32[4,4,128,128]{3,2,1,0:T(8,128)S(1)}, f32[4,4,128,128]{3,2,1,0:T(8,128)S(1)}, u32[]{:S(2)}, u32[]{:S(2)}) collective-permute-start(f32[4,4,128,128]{3,2,1,0:T(8,128)S(1)} %all_to_all.28.own_ref), channel_id=1, source_target_pairs={{0,1},{1,0},{2,3},{3,2},{4,5},{5,4},{6,7},{7,6},{8,9},{9,8},{10,11... | collective-permute-start | bytes 3145736 | tf_op jit(solution)/shard_map/ppermute | solution.py:286
